TPU v7x, 256 devices: a whole 4x4x8 slice. The times are simulated.
256 devices in a mesh: blk: 64 (over x_lo, y, z), sec: 4 (over x_hi, core).
Axes of the slice: x: 4 (x_hi: 2, x_lo: 2; x = x_hi * 2 + x_lo), y: 4, z: 8, core: 2. Of those that a mesh axis runs over, the one named last changes fastest.
Arguments:
- factors: bfloat16 [64, 512, 1024], P('blk', None, 'sec'), may hold values from -0.5 to 0.5
- occ_energy: float32 [64], replicated, may hold values from -2 to -0.5
- vir_energy: float32 [512], replicated, may hold values from 0.2 to 3
- metric: float32 [1024, 1024], replicated, may hold values from -0.1875 to 0.1875
Outputs:
- gamma: float32 [1024, 64, 512], P('sec', 'blk')
- density: float32 [512, 512], P('blk')
All inputs are finite; a program needn't handle non-finite values.
Results may differ from a plain program's by a relative error of at most 0.00077.
Values may be sent and summed in bfloat16 or wider, within the bound.
A program may use at most 64 MiB of HBM per device.

v0:
```python
import jax
import jax.numpy as jnp
from jax import lax
from jax.sharding import PartitionSpec as P

CYCLE_STEPS = 4


def from_behind(shard, axis, by):
    devices = lax.axis_size(axis)
    return lax.ppermute(shard, axis, [(i, (i + by) % devices) for i in range(devices)])


def batch_energy(occ_energy, batch_index, per_batch):
    return lax.dynamic_slice_in_dim(occ_energy, batch_index * per_batch, per_batch, 0)


def pair_block(
    own_full, own_energy, partner, part_energy, vir_energy, acc_own, acc_part, density, weight
):
    per_batch = own_full.shape[0]

    def one_pair(pair_index, loop_state):
        acc_own, acc_part, density = loop_state
        first_pos = pair_index // per_batch
        second = pair_index % per_batch
        left_block = lax.dynamic_index_in_dim(own_full, first_pos, 0, keepdims=False)
        right_block = lax.dynamic_index_in_dim(partner, second, 0, keepdims=False)
        intersection = lax.dot_general(
            left_block, right_block, (((1,), (1,)), ((), ())), preferred_element_type=jnp.float32
        )
        energy_sum = lax.dynamic_index_in_dim(
            own_energy, first_pos, 0, keepdims=False
        ) + lax.dynamic_index_in_dim(part_energy, second, 0, keepdims=False)
        denominator = energy_sum - vir_energy[:, None] - vir_energy[None, :]
        amplitude = intersection / denominator
        mixed_amp = 2.0 * amplitude - amplitude.T
        amp_half = amplitude.astype(jnp.bfloat16)
        mixed_half = mixed_amp.astype(jnp.bfloat16)
        own_term = jnp.einsum(
            "bp,ab->pa", right_block, mixed_half, preferred_element_type=jnp.float32
        )
        acc_own = acc_own.at[first_pos].add(weight * own_term)
        dens_term = lax.dot_general(
            mixed_half, amp_half, (((1,), (1,)), ((), ())), preferred_element_type=jnp.float32
        )
        part_term = jnp.einsum(
            "ap,ab->pb", left_block, mixed_half, preferred_element_type=jnp.float32
        )
        acc_part = acc_part.at[second].add(weight * part_term)
        dens_term = dens_term + lax.dot_general(
            mixed_half, amp_half, (((0,), (0,)), ((), ())), preferred_element_type=jnp.float32
        )
        density = density + weight * dens_term
        return (acc_own, acc_part, density)

    return lax.fori_loop(0, per_batch * per_batch, one_pair, (acc_own, acc_part, density))


def per_device(factors, occ_energy, vir_energy, metric):
    n_blk = lax.axis_size("blk")
    n_sec = lax.axis_size("sec")
    blk_pos = lax.axis_index("blk")
    sec_pos = lax.axis_index("sec")
    per_batch = factors.shape[0]
    virtuals = factors.shape[1]
    aux_part = factors.shape[2]
    aux_total = aux_part * n_sec
    cycle_turns = min(CYCLE_STEPS, n_blk // (2 * n_sec))
    own_full = lax.all_gather(factors, "sec", axis=2, tiled=True)
    own_energy = batch_energy(occ_energy, blk_pos, per_batch)
    acc_own = jnp.zeros((per_batch, aux_total, virtuals), jnp.float32)
    density = jnp.zeros((virtuals, virtuals), jnp.float32)
    segmented = [factors]
    moving = factors
    for shift_turn in range(n_sec - 1):
        moving = from_behind(moving, "blk", 1)
        segmented.append(moving)
    partner = lax.all_to_all(
        jnp.stack(segmented, 0), "sec", split_axis=0, concat_axis=3, tiled=True
    )[0]
    acc_part = jnp.zeros((per_batch, aux_total, virtuals), jnp.float32)
    for cycle_step in range(cycle_turns):
        if cycle_step > 0:
            partner = from_behind(partner, "blk", n_sec)
            acc_part = from_behind(acc_part, "blk", n_sec)
        offset = sec_pos + n_sec * cycle_step
        weight = jnp.where(offset == 0, jnp.float32(0.5), jnp.float32(1.0))
        part_energy = batch_energy(occ_energy, (blk_pos - offset) % n_blk, per_batch)
        acc_own, acc_part, density = pair_block(
            own_full,
            own_energy,
            partner,
            part_energy,
            vir_energy,
            acc_own,
            acc_part,
            density,
            weight,
        )
    acc_part = from_behind(acc_part, "blk", -n_sec * (cycle_turns - 1))
    regrouped = lax.all_to_all(acc_part[None], "sec", split_axis=2, concat_axis=0, tiled=True)
    carried = regrouped[n_sec - 1]
    for shift_turn in range(n_sec - 2, -1, -1):
        carried = from_behind(carried, "blk", -1) + regrouped[shift_turn]
    metric_rows = lax.dynamic_slice_in_dim(metric, sec_pos * aux_part, aux_part, 0)
    own_term = jnp.einsum("pq,ipa->qia", metric, acc_own, precision=lax.Precision.HIGHEST)
    gamma_part = lax.psum_scatter(
        own_term + jnp.einsum("pq,ipa->qia", metric_rows, carried, precision=lax.Precision.HIGHEST),
        "sec",
        scatter_dimension=0,
        tiled=True,
    )
    row_count = virtuals // n_blk
    density_all = lax.psum(density, ("blk", "sec"))
    density_out = lax.dynamic_slice_in_dim(density_all, blk_pos * row_count, row_count, 0)
    return (gamma_part, density_out)


def solution(mesh):
    return jax.shard_map(
        per_device,
        mesh=mesh,
        in_specs=(P("blk", None, "sec"), P(), P(), P()),
        out_specs=(P("sec", "blk", None), P("blk", None)),
        check_vma=False,
    )
```

profile of v0, /device:TPU:1, one launch (start us, length us, event | category | flops | bytes accessed | tf_op | source)
XLA Modules:
  0.0 949.6 jit_solution(4320197926816202612)
XLA Ops:
  8.3 2.5 collective-permute-start
  10.8 13.3 %collective-permute-done = bf16[1,512,256]{1,2,0:T(8,128)(2,1)S(1)} collective-permute-done((bf16[1,512,256]{1,2,0:T(8,128)(2,1)S(1)}, bf16[1,512,256]{1,2,0:T(8,128)(2,1)S(1)}, u32[]{:S(2)}, u32[]{:S(2)}) %collective-permute-start) | collective-permute-done | bytes 262176 | tf_op jit(solution)/shard_map/ppermute | solution.py:11
  24.2 10.8 %collective-permute-done.1 = bf16[1,512,256]{1,2,0:T(8,128)(2,1)S(1)} collective-permute-done((bf16[1,512,256]{1,2,0:T(8,128)(2,1)S(1)}, bf16[1,512,256]{1,2,0:T(8,128)(2,1)S(1)}, u32[]{:S(2)}, u32[]{:S(2)}) %collective-permute-start.1) | collective-permute-done | bytes 262176 | tf_op jit(solution)/shard_map/ppermute | solution.py:11
  35.0 10.0 %collective-permute-done.2 = bf16[1,512,256]{1,2,0:T(8,128)(2,1)S(1)} collective-permute-done((bf16[1,512,256]{1,2,0:T(8,128)(2,1)S(1)}, bf16[1,512,256]{1,2,0:T(8,128)(2,1)S(1)}, u32[]{:S(2)}, u32[]{:S(2)}) %collective-permute-start.2) | collective-permute-done | bytes 262176 | tf_op jit(solution)/shard_map/ppermute | solution.py:11
  45.1 21.7 %all_to_all.27 = bf16[4,1,512,256]{2,3,1,0:T(8,128)(2,1)S(1)} all-to-all(bf16[4,1,512,256]{2,3,1,0:T(8,128)(2,1)S(1)} %pad_maximum_fusion), channel_id=1, replica_groups=mesh['blk'=64,'sec'=4] {'sec'}, dimensions={0} | all-to-all | bytes 2097152 | tf_op jit(solution)/shard_map/all_to_all | solution.py:79
  66.8 45.5 %collective-permute-done.3 = bf16[1,512,1024]{1,2,0:T(8,128)(2,1)S(1)} collective-permute-done((bf16[1,512,1024]{1,2,0:T(8,128)(2,1)S(1)}, bf16[1,512,1024]{1,2,0:T(8,128)(2,1)S(1)}, u32[]{:S(2)}, u32[]{:S(2)}) %collective-permute-start.3) | collective-permute-done | bytes 1048608 | tf_op jit(solution)/shard_map/ppermute | solution.py:11
  118.2 41.9 %collective-permute-done.4 = bf16[1,512,1024]{1,2,0:T(8,128)(2,1)} collective-permute-done((bf16[1,512,1024]{1,2,0:T(8,128)(2,1)S(1)}, bf16[1,512,1024]{1,2,0:T(8,128)(2,1)}, u32[]{:S(2)}, u32[]{:S(2)}) %collective-permute-start.4) | collective-permute-done | bytes 1048608 | tf_op jit(solution)/shard_map/ppermute | solution.py:11
  160.2 2.1 fusion.37
  162.3 1.3 copy.26
  163.6 3.0 fusion.26
  166.6 2.5 copy.27
  169.1 2.0 fusion.22
  171.1 1.3 copy.28
  172.4 34.9 %collective-permute-done.5 = bf16[1,512,1024]{1,2,0:T(8,128)(2,1)} collective-permute-done((bf16[1,512,1024]{1,2,0:T(8,128)(2,1)}, bf16[1,512,1024]{1,2,0:T(8,128)(2,1)}, u32[]{:S(2)}, u32[]{:S(2)}) %collective-permute-start.5) | collective-permute-done | bytes 1048608 | tf_op jit(solution)/shard_map/ppermute | solution.py:11
  207.3 2.0 fusion.18
  209.3 1.4 copy.29
  210.6 4.2 subtract_convert_fusion.3
  214.8 2.1 multiply_bitcast_fusion
  216.9 83.0 %collective-permute-done.6 = f32[1,1024,512]{1,2,0:T(8,128)} collective-permute-done((f32[1,1024,512]{1,2,0:T(8,128)}, f32[1,1024,512]{1,2,0:T(8,128)}, u32[]{:S(2)}, u32[]{:S(2)}) %collective-permute-start.6) | collective-permute-done | bytes 2097184 | tf_op jit(solution)/shard_map/ppermute | solution.py:11
  299.9 3.7 bitcast_add_fusion.2
  304.3 87.8 %collective-permute-done.7 = f32[1,1024,512]{1,2,0:T(8,128)} collective-permute-done((f32[1,1024,512]{1,2,0:T(8,128)}, f32[1,1024,512]{1,2,0:T(8,128)}, u32[]{:S(2)}, u32[]{:S(2)}) %collective-permute-start.7) | collective-permute-done | bytes 2097184 | tf_op jit(solution)/shard_map/ppermute | solution.py:11
  392.1 3.4 bitcast_add_fusion.1
  396.2 88.8 %collective-permute-done.8 = f32[1,1024,512]{1,2,0:T(8,128)} collective-permute-done((f32[1,1024,512]{1,2,0:T(8,128)}, f32[1,1024,512]{1,2,0:T(8,128)}, u32[]{:S(2)}, u32[]{:S(2)}) %collective-permute-start.8) | collective-permute-done | bytes 2097184 | tf_op jit(solution)/shard_map/ppermute | solution.py:11
  484.9 3.4 bitcast_add_fusion
  490.1 1.6 fusion.56
  491.7 1.6 fusion.53
  493.3 1.5 fusion.15
  494.8 77.9 %collective-permute-done.9 = f32[1,1024,512]{1,2,0:T(8,128)} collective-permute-done((f32[1,1024,512]{1,2,0:T(8,128)}, f32[1,1024,512]{1,2,0:T(8,128)}, u32[]{:S(2)}, u32[]{:S(2)}) %collective-permute-start.9) | collective-permute-done | bytes 2097184 | tf_op jit(solution)/shard_map/ppermute | solution.py:11
  572.8 6.0 copy.30
  578.8 4.1 all-to-all-start.1
  582.9 2.0 fusion.50
  588.0 1.5 fusion.10
  589.6 3.4 fusion.64
  593.0 16.1 %all-to-all-done.1 = f32[1,1,1024,512]{3,1,0,2:T(1,128)S(1)} async-done(((f32[1,1,1024,512]{3,1,0,2:T(1,128)}), f32[1,1,1024,512]{3,1,0,2:T(1,128)S(1)}, u32[]{:S(2)}, u32[]{:S(2)}) %all-to-all-start.1) | async-done | bytes 2097184 | tf_op jit(solution)/shard_map/all_to_all | solution.py:102
  609.3 39.6 %collective-permute-start.10 = (f32[1,256,512]{2,1,0:T(8,128)S(1)}, f32[1,256,512]{2,1,0:T(8,128)S(1)}, u32[]{:S(2)}, u32[]{:S(2)}) collective-permute-start(f32[1,256,512]{2,1,0:T(8,128)S(1)} %slice_bitcast_fusion), channel_id=1, source_target_pairs={{0,252},{4,0},{8,4},{12,8},{16,12},{20,16},{24,20},{28,24},{32,28}... | collective-permute-start | bytes 1572872 | tf_op jit(solution)/shard_map/ppermute | solution.py:11
  650.7 9.0 collective-permute-done.10
  659.8 6.8 collective-permute-start.11
  666.5 2.1 fusion.20
  668.7 2.1 fusion.16
  670.8 5.8 collective-permute-done.11
  676.6 6.5 collective-permute-start.12
  683.1 7.3 fusion.1
  690.4 2.0 collective-permute-done.12
  692.4 3.3 fusion
  695.7 199.3 %all-reduce.2.cloned.1.call-done = f32[512,512]{1,0:T(8,128)} async-done(((f32[512,512]{1,0:T(8,128)}), f32[512,512]{1,0:T(8,128)}) %all-reduce.2.cloned.1.call-update) | async-done | bytes 1048592 | tf_op jit(solution)/shard_map/psum | solution.py:115
  895.0 1.3 constant_dynamic-slice_fusion
  896.3 44.9 %reduce-scatter.2.cloned.1.call-done = f32[256,1,512]{0,2,1:T(8,128)} async-done(((f32[1024,1,512]{0,2,1:T(8,128)}), f32[256,1,512]{0,2,1:T(8,128)}) %reduce-scatter.2.cloned.1.call-update) | async-done | bytes 524304 | tf_op jit(solution)/shard_map/reduce_scatter | solution.py:108
  941.2 1.9 copy.35
  (81 shorter events, 10.7 us)
Async XLA Ops:
  7.2 153.0 %all-gather.2.cloned.1.call-start = ((), (), s32[]{:S(2)}) async-start(), calls=%async_computation.3 | async-start | bytes 1310720 | tf_op jit(solution)/shard_map/all_gather | solution.py:70
  8.3 15.9 %collective-permute-start = (bf16[1,512,256]{1,2,0:T(8,128)(2,1)S(1)}, bf16[1,512,256]{1,2,0:T(8,128)(2,1)S(1)}, u32[]{:S(2)}, u32[]{:S(2)}) collective-permute-start(bf16[1,512,256]{1,2,0:T(8,128)(2,1)S(1)} %copy.24), channel_id=1, source_target_pairs={{0,4},{4,8},{8,12},{12,16},{16,20},{20,24},{24,28},{28,32},{32,36}... | collective-permute-start | bytes 786440 | tf_op jit(solution)/shard_map/ppermute | solution.py:11
  24.2 10.8 %collective-permute-start.1 = (bf16[1,512,256]{1,2,0:T(8,128)(2,1)S(1)}, bf16[1,512,256]{1,2,0:T(8,128)(2,1)S(1)}, u32[]{:S(2)}, u32[]{:S(2)}) collective-permute-start(bf16[1,512,256]{1,2,0:T(8,128)(2,1)S(1)} %collective-permute-done), channel_id=1, source_target_pairs={{0,4},{4,8},{8,12},{12,16},{16,20},{20,24},{24,28},{28,32},{32,36}... | collective-permute-start | bytes 786440 | tf_op jit(solution)/shard_map/ppermute | solution.py:11
  35.0 10.0 %collective-permute-start.2 = (bf16[1,512,256]{1,2,0:T(8,128)(2,1)S(1)}, bf16[1,512,256]{1,2,0:T(8,128)(2,1)S(1)}, u32[]{:S(2)}, u32[]{:S(2)}) collective-permute-start(bf16[1,512,256]{1,2,0:T(8,128)(2,1)S(1)} %collective-permute-done.1), channel_id=1, source_target_pairs={{0,4},{4,8},{8,12},{12,16},{16,20},{20,24},{24,28},{28,32},{32,36}... | collective-permute-start | bytes 786440 | tf_op jit(solution)/shard_map/ppermute | solution.py:11
  45.0 67.4 %copy-start.21 = (f32[64]{0:T(128)S(1)}, f32[64]{0:T(128)}, u32[]{:S(2)}) copy-start(f32[64]{0:T(128)} %param.21) | copy-start | bytes 772
  45.0 115.2 %copy-start.20 = (f32[512]{0:T(512)S(1)}, f32[512]{0:T(512)}, u32[]{:S(2)}) copy-start(f32[512]{0:T(512)} %param.22) | copy-start | bytes 6148
  66.8 96.8 %copy-start.7 = (bf16[4,1,512,256]{2,3,1,0:T(8,128)(2,1)}, bf16[4,1,512,256]{2,3,1,0:T(8,128)(2,1)S(1)}, u32[]{:S(2)}) copy-start(bf16[4,1,512,256]{2,3,1,0:T(8,128)(2,1)S(1)} %all_to_all.27) | copy-start | bytes 3145732
  66.8 45.6 %collective-permute-start.3 = (bf16[1,512,1024]{1,2,0:T(8,128)(2,1)S(1)}, bf16[1,512,1024]{1,2,0:T(8,128)(2,1)S(1)}, u32[]{:S(2)}, u32[]{:S(2)}) collective-permute-start(bf16[1,512,1024]{1,2,0:T(8,128)(2,1)S(1)} %bitcast.150), channel_id=1, source_target_pairs={{0,16},{4,20},{8,24},{12,28},{16,32},{20,36},{24,40},{28,44},{32,4... | collective-permute-start | bytes 3145736 | tf_op jit(solution)/shard_map/ppermute | solution.py:11
  112.3 47.9 %copy-start.18 = (bf16[1,512,1024]{1,2,0:T(8,128)(2,1)}, bf16[1,512,1024]{1,2,0:T(8,128)(2,1)S(1)}, u32[]{:S(2)}) copy-start(bf16[1,512,1024]{1,2,0:T(8,128)(2,1)S(1)} %collective-permute-done.3) | copy-start | bytes 3145732
  112.3 47.8 %collective-permute-start.4 = (bf16[1,512,1024]{1,2,0:T(8,128)(2,1)S(1)}, bf16[1,512,1024]{1,2,0:T(8,128)(2,1)}, u32[]{:S(2)}, u32[]{:S(2)}) collective-permute-start(bf16[1,512,1024]{1,2,0:T(8,128)(2,1)S(1)} %collective-permute-done.3), channel_id=1, source_target_pairs={{0,16},{4,20},{8,24},{12,28},{16,32},{20,36},{24,40},{28,44},{32,4... | collective-permute-start | bytes 3145736 | tf_op jit(solution)/shard_map/ppermute | solution.py:11
  160.1 47.1 %collective-permute-start.5 = (bf16[1,512,1024]{1,2,0:T(8,128)(2,1)}, bf16[1,512,1024]{1,2,0:T(8,128)(2,1)}, u32[]{:S(2)}, u32[]{:S(2)}) collective-permute-start(bf16[1,512,1024]{1,2,0:T(8,128)(2,1)} %collective-permute-done.4), channel_id=1, source_target_pairs={{0,16},{4,20},{8,24},{12,28},{16,32},{20,36},{24,40},{28,44},{32,4... | collective-permute-start | bytes 3145736 | tf_op jit(solution)/shard_map/ppermute | solution.py:11
  160.2 3.4 copy-start
  162.3 4.3 copy-start.15
  171.1 38.2 %copy-start.16 = (f32[512,512]{1,0:T(8,128)}, f32[512,512]{1,0:T(8,128)S(1)}, u32[]{:S(2)}) copy-start(f32[512,512]{1,0:T(8,128)S(1)} %fusion.22) | copy-start | bytes 3145732
  209.3 1.4 copy-start.17
  214.8 274.7 %copy-start.3 = (bf16[512,512]{1,0:T(8,128)(2,1)}, bf16[512,512]{1,0:T(8,128)(2,1)S(1)}, u32[]{:S(2)}) copy-start(bf16[512,512]{1,0:T(8,128)(2,1)S(1)} %get-tuple-element.280) | copy-start | bytes 1572868
  214.8 278.5 %copy-start.6 = (bf16[512,512]{1,0:T(8,128)(2,1)}, bf16[512,512]{1,0:T(8,128)(2,1)S(1)}, u32[]{:S(2)}) copy-start(bf16[512,512]{1,0:T(8,128)(2,1)S(1)} %get-tuple-element.279) | copy-start | bytes 1572868
  216.9 83.0 %collective-permute-start.6 = (f32[1,1024,512]{1,2,0:T(8,128)}, f32[1,1024,512]{1,2,0:T(8,128)}, u32[]{:S(2)}, u32[]{:S(2)}) collective-permute-start(f32[1,1024,512]{1,2,0:T(8,128)} %multiply_bitcast_fusion), channel_id=1, source_target_pairs={{0,16},{4,20},{8,24},{12,28},{16,32},{20,36},{24,40},{28,44},{32,4... | collective-permute-start | bytes 6291464 | tf_op jit(solution)/shard_map/ppermute | solution.py:11
  303.6 88.5 %collective-permute-start.7 = (f32[1,1024,512]{1,2,0:T(8,128)}, f32[1,1024,512]{1,2,0:T(8,128)}, u32[]{:S(2)}, u32[]{:S(2)}) collective-permute-start(f32[1,1024,512]{1,2,0:T(8,128)} %bitcast_add_fusion.2), channel_id=1, source_target_pairs={{0,16},{4,20},{8,24},{12,28},{16,32},{20,36},{24,40},{28,44},{32,4... | collective-permute-start | bytes 6291464 | tf_op jit(solution)/shard_map/ppermute | solution.py:11
  395.4 89.5 %collective-permute-start.8 = (f32[1,1024,512]{1,2,0:T(8,128)}, f32[1,1024,512]{1,2,0:T(8,128)}, u32[]{:S(2)}, u32[]{:S(2)}) collective-permute-start(f32[1,1024,512]{1,2,0:T(8,128)} %bitcast_add_fusion.1), channel_id=1, source_target_pairs={{0,16},{4,20},{8,24},{12,28},{16,32},{20,36},{24,40},{28,44},{32,4... | collective-permute-start | bytes 6291464 | tf_op jit(solution)/shard_map/ppermute | solution.py:11
  396.2 92.7 %copy-start.13 = (f32[512,512]{0,1:T(8,128)S(1)}, f32[512,512]{0,1:T(8,128)}, u32[]{:S(2)}) copy-start(f32[512,512]{0,1:T(8,128)} %copy.26) | copy-start | bytes 3145732
  488.3 84.5 %collective-permute-start.9 = (f32[1,1024,512]{1,2,0:T(8,128)}, f32[1,1024,512]{1,2,0:T(8,128)}, u32[]{:S(2)}, u32[]{:S(2)}) collective-permute-start(f32[1,1024,512]{1,2,0:T(8,128)} %bitcast_add_fusion), channel_id=1, source_target_pairs={{0,208},{4,212},{8,216},{12,220},{16,224},{20,228},{24,232},{28,23... | collective-permute-start | bytes 6291464 | tf_op jit(solution)/shard_map/ppermute | solution.py:11
  488.9 1.2 copy-start.11
  490.1 1.6 copy-start.8
  491.7 1.6 copy-start.14
  578.8 30.3 %all-to-all-start.1 = ((f32[1,1,1024,512]{3,1,0,2:T(1,128)}), f32[1,1,1024,512]{3,1,0,2:T(1,128)S(1)}, u32[]{:S(2)}, u32[]{:S(2)}) async-start(f32[1,1,1024,512]{3,1,0,2:T(1,128)} %copy.30), calls=%async_computation.1 | async-start | bytes 4194304 | tf_op jit(solution)/shard_map/all_to_all | solution.py:102
  582.9 312.1 %all-reduce.2.cloned.1.call-start = ((), (), s32[]{:S(2)}) async-start(), calls=%async_computation.5 | async-start | bytes 2097152 | tf_op jit(solution)/shard_map/psum | solution.py:115
  582.9 2.0 copy-start.4
  582.9 2.0 copy-start.12
  582.9 2.0 copy-start.23
  582.9 2.3 copy-start.24
  585.2 1.2 copy-start.9
  585.2 1.5 copy-start.22
  586.8 1.2 copy-start.10
  589.5 351.7 %reduce-scatter.2.cloned.1.call-start = ((), (), s32[]{:S(2)}) async-start(), calls=%async_computation.4 | async-start | bytes 2621440 | tf_op jit(solution)/shard_map/reduce_scatter | solution.py:108
  609.1 39.8 %copy-start.5 = (bf16[512,512]{1,0:T(8,128)(2,1)S(1)}, bf16[512,512]{1,0:T(8,128)(2,1)}, u32[]{:S(2)}) copy-start(bf16[512,512]{1,0:T(8,128)(2,1)} %copy-done.3) | copy-start | bytes 1572868
  609.1 39.8 %copy-start.19 = (bf16[1,512,1024]{1,2,0:T(8,128)(2,1)S(1)}, bf16[1,512,1024]{1,2,0:T(8,128)(2,1)}, u32[]{:S(2)}) copy-start(bf16[1,512,1024]{1,2,0:T(8,128)(2,1)} %copy-done.18) | copy-start | bytes 3145732
  609.3 50.4 %collective-permute-start.10 = (f32[1,256,512]{2,1,0:T(8,128)S(1)}, f32[1,256,512]{2,1,0:T(8,128)S(1)}, u32[]{:S(2)}, u32[]{:S(2)}) collective-permute-start(f32[1,256,512]{2,1,0:T(8,128)S(1)} %slice_bitcast_fusion), channel_id=1, source_target_pairs={{0,252},{4,0},{8,4},{12,8},{16,12},{20,16},{24,20},{28,24},{32,28}... | collective-permute-start | bytes 1572872 | tf_op jit(solution)/shard_map/ppermute | solution.py:11
  659.8 16.8 %collective-permute-start.11 = (f32[1,256,512]{2,1,0:T(8,128)S(1)}, f32[1,256,512]{2,1,0:T(8,128)S(1)}, u32[]{:S(2)}, u32[]{:S(2)}) collective-permute-start(f32[1,256,512]{2,1,0:T(8,128)S(1)} %fusion.48), channel_id=1, source_target_pairs={{0,252},{4,0},{8,4},{12,8},{16,12},{20,16},{24,20},{28,24},{32,28}... | collective-permute-start | bytes 1572872 | tf_op jit(solution)/shard_map/ppermute | solution.py:11
  666.5 16.6 %copy-start.2 = (f32[1024,1024]{1,0:T(8,128)S(1)}, f32[1024,1024]{1,0:T(8,128)}, u32[]{:S(2)}) copy-start(f32[1024,1024]{1,0:T(8,128)} %param.23) | copy-start | bytes 12582916
  668.7 14.5 %copy-start.1 = (f32[1024,512]{1,0:T(8,128)S(1)}, f32[1024,512]{1,0:T(8,128)}, u32[]{:S(2)}) copy-start(f32[1024,512]{1,0:T(8,128)} %fusion.64) | copy-start | bytes 6291460
  676.6 15.8 %collective-permute-start.12 = (f32[1,256,512]{2,1,0:T(8,128)S(1)}, f32[1,256,512]{2,1,0:T(8,128)S(1)}, u32[]{:S(2)}, u32[]{:S(2)}) collective-permute-start(f32[1,256,512]{2,1,0:T(8,128)S(1)} %fusion.47), channel_id=1, source_target_pairs={{0,252},{4,0},{8,4},{12,8},{16,12},{20,16},{24,20},{28,24},{32,28}... | collective-permute-start | bytes 1572872 | tf_op jit(solution)/shard_map/ppermute | solution.py:11
Sparse Core Ops, SparseCore 0:
  66.9 23.7 all-gather.1
  589.7 305.3 all-reduce.1
  897.8 43.3 reduce-scatter.1
where the time goes:
time: 951 us; the launch traced here: 950 us
  waiting for transfers between devices  771 us (81%)
  starting transfers between devices  60.1 us (6%)
  matrix products  45.1 us (5%)
  blocking collectives  21.7 us (2%)
  local copies, waits for them, and re-layouts  21.6 us (2%)
  between operations  19.1 us (2%)
  other arithmetic  11.2 us (1%)
    ppermute x13, waiting for transfers between devices, from_behind(): lax.ppermute(shard, axis, [(i, (i + by) % devices) for i in range(devices)])  511 us
    psum x1, waiting for transfers between devices, per_device(): density_all = lax.psum(density, ('blk', 'sec'))  199 us
    ppermute x13, starting transfers between devices, from_behind(): lax.ppermute(shard, axis, [(i, (i + by) % devices) for i in range(devices)])  56 us
    reduce_scatter x1, waiting for transfers between devices, per_device(): lax.psum_scatter(own_term + jnp.einsum('pq,ipa->qia', metric_rows, carrie...  44.9 us
    all_to_all x1, blocking collectives, per_device(): lax.all_to_all(jnp.stack(segmented, 0), 'sec', split_axis=0, concat_axis=...  21.7 us
  transfers between devices with their start and end apart: 17, of which 16 were waited for; matrix products, arithmetic and copies ran while one was open for 5% of the time, Pallas kernels for 0%

commit v1 on v0

v1 whole, which is shorter than its diff:
```python
import jax
import jax.numpy as jnp
from jax import lax
from jax.experimental import pallas as pl
from jax.experimental.pallas import tpu as pltpu
from jax.sharding import PartitionSpec as P

MESH = pl.DeviceIdType.MESH
F32 = jnp.float32
BF16 = jnp.bfloat16
NT = (((1,), (1,)), ((), ()))
NN = (((1,), (0,)), ((), ()))

V = 512
QW = 256
NB = 64
STEPS = 8
ROWS = 256


def dot(a, b, dims):
    return lax.dot_general(a, b, dims, preferred_element_type=F32)


def kernel(
    occ_ref,
    f_ref,
    vir_ref,
    metric_ref,
    gamma_ref,
    dens_out_ref,
    slots,
    g_acc,
    dens,
    vir_sum,
    t_buf,
    tb_buf,
    m_f32,
    m_hi,
    m_lo,
    g_hi,
    g_lo,
    part,
    ra,
    rb,
    rx,
    dr0,
    d1,
    dry,
    d2,
    drz,
    d3,
    drx,
    d4,
    dr4,
    local_sem,
    init_ssem,
    ssem,
    rsem,
    tail_ssem,
    tail_rsem,
    y_ssem,
    y_rsem,
    z_ssem,
    z_rsem,
    x_ssem,
    x_rsem,
):
    b = lax.axis_index("blk")
    s = lax.axis_index("sec")
    x_hi = s // 2
    core = s % 2
    x_lo = b // 32
    y = (b // 8) % 4
    z = b % 8
    far = s // 2
    mate = s + 1 - 2 * core
    across = (s + 2) % 4
    diag = 3 - s
    sign = 1 - 2 * core
    nxt = (b + sign + NB) % NB
    prv = (b - sign + NB) % NB

    def y_peer(i):
        yy = (y + i) % 4
        return yy, (x_lo * 32 + yy * 8 + z, s)

    def z_peer(i):
        zz = (z + i) % 8
        return zz, (x_lo * 32 + y * 8 + zz, s)

    def x_peer(i):
        xx = (x_hi * 2 + x_lo + i) % 4
        return xx, ((xx % 2) * 32 + y * 8 + z, (xx // 2) * 2 + core)

    barrier = pltpu.get_barrier_semaphore()

    def greet(dev):
        pl.semaphore_signal(barrier, inc=1, device_id=dev, device_id_type=MESH)

    for t in (mate, across, diag):
        greet((b, t))
    greet((nxt, s))
    greet((prv, s))
    greet(((b + 8) % NB, 2))
    greet(((b + NB - 8) % NB, 3))

    @pl.when(far == 1)
    def _():
        source = (b - 8 * sign + NB) % NB
        for t in range(4):
            greet((source, t))

    for i in (1, 2, 3):
        greet(y_peer(i)[1])
    for i in range(1, 8):
        greet(z_peer(i)[1])
    for i in (1, 3):
        greet(x_peer(i)[1])

    metric_copy = pltpu.make_async_copy(metric_ref, m_f32, local_sem.at[1])
    metric_copy.start()
    own_copy = pltpu.make_async_copy(f_ref.at[0], slots.at[0, s], local_sem.at[0])
    own_copy.start()

    pl.semaphore_wait(barrier, 19 + 4 * far)

    def remote(src, dst, send, recv, dev):
        return pltpu.make_async_remote_copy(
            src_ref=src, dst_ref=dst, send_sem=send, recv_sem=recv,
            device_id=dev, device_id_type=MESH,
        )

    firsts = []
    for i, (dev, entry) in enumerate(
        (
            ((b, across), 0),
            ((b, mate), 0),
            ((b, diag), 0),
            (((b + 8) % NB, 2), 8),
            (((b + NB - 8) % NB, 3), 8),
        )
    ):
        c = remote(f_ref.at[0], slots.at[entry, s], init_ssem.at[i], rsem.at[entry, s], dev)
        c.start()
        firsts.append(c)

    def hop(src_entry, dst_entry, q):
        return remote(
            slots.at[src_entry, q], slots.at[dst_entry, q],
            ssem.at[dst_entry, q], rsem.at[dst_entry, q], (nxt, s),
        )

    def arrived(entry, q):
        remote(
            slots.at[entry, q], slots.at[entry, q],
            ssem.at[entry, q], rsem.at[entry, q], (nxt, s),
        ).wait_recv()

    order = (s, mate, across, diag)

    own_copy.wait()

    @pl.when(far == 0)
    def _():
        for n, q in enumerate(order):
            if n > 0:
                arrived(0, q)
            hop(0, 1, q).start()

    @pl.when(far == 1)
    def _():
        for q in order:
            arrived(8, q)
            hop(8, 1, q).start()
        for q in order[1:]:
            arrived(0, q)

    vir_rows = jnp.broadcast_to(vir_ref[...], (V, V))
    vir_sum[...] = vir_rows + vir_rows.T
    g_acc[...] = jnp.zeros_like(g_acc)
    dens[...] = jnp.zeros_like(dens)
    metric_copy.wait()
    for i in range(4):
        rows = pl.ds(i * QW, QW)
        m = m_f32[rows, :]
        hi = m.astype(BF16)
        m_hi[rows, :] = hi
        m_lo[rows, :] = (m - hi.astype(F32)).astype(BF16)

    own_e = occ_ref[b]

    def pair(entry, offset):
        e_sum = own_e + occ_ref[(b - sign * offset + 2 * NB) % NB]
        for rc in range(V // ROWS):
            rows = pl.ds(rc * ROWS, ROWS)
            acc = dot(slots[0, 0, rows, :], slots[entry, 0], NT)
            for q in range(1, 4):
                acc = acc + dot(slots[0, q, rows, :], slots[entry, q], NT)
            t = acc / (e_sum - vir_sum[rows, :])
            t_buf[rows, :] = t
            tb_buf[rows, :] = t.astype(BF16)
        for rc in range(V // ROWS):
            rows = pl.ds(rc * ROWS, ROWS)
            ub = (2.0 * t_buf[rows, :] - t_buf[:, rows].T).astype(BF16)
            for q in range(4):
                g_acc[q, rows, :] += dot(ub, slots[entry, q], NN)
            for h in range(2):
                dens[h, rows, :] += dot(ub, tb_buf[pl.ds(h * QW, QW), :], NT)

    @pl.when(s != 1)
    def _():
        pair(8 * far, 8 * far)

    def step(k, carry):
        for q in order:
            arrived(k, q)

            @pl.when(k < STEPS - 1)
            def _():
                hop(k, k + 1, q).start()

        pair(k, k + 8 * far)
        return carry

    lax.fori_loop(1, STEPS, step, 0)

    sends = []

    def send(src, dst, ss, rs, dev):
        c = remote(src, dst, ss, rs, dev)
        c.start()
        sends.append(c)
        return c

    c_d0 = send(dens.at[1 - core], dr0, tail_ssem.at[0], tail_rsem.at[0], (b, mate))

    for q in range(4):
        g = g_acc[q]
        hi = g.astype(BF16)
        g_hi[q] = hi
        g_lo[q] = (g - hi.astype(F32)).astype(BF16)

    def metric_part(t):
        cols = pl.ds(pl.multiple_of(t * QW, QW), QW)
        acc = None
        for q in range(4):
            rows = pl.ds(q * QW, QW)
            mh = m_hi[rows, cols]
            ml = m_lo[rows, cols]
            term = dot(g_hi[q], mh, NN) + (dot(g_lo[q], mh, NN) + dot(g_hi[q], ml, NN))
            acc = term if acc is None else acc + term
        return acc

    part[0] = metric_part(diag)
    c_a = send(part.at[0], ra, tail_ssem.at[1], tail_rsem.at[1], (b, mate))

    c_d0.wait_recv()
    for xl in range(2):
        for yy in range(4):
            rows = pl.ds(xl * 256 + yy * 64, 64)
            d1[yy, xl] = dens[core, rows, :] + dr0[rows, :]
    y_copies = []
    for i in (1, 2, 3):
        yy, dev = y_peer(i)
        y_copies.append(send(d1.at[yy], dry.at[y], y_ssem.at[i], y_rsem.at[y], dev))

    p_across = metric_part(across)
    c_a.wait_recv()
    part[1] = p_across + ra[...]
    c_x = send(part.at[1], rx, tail_ssem.at[2], tail_rsem.at[2], (b, across))

    part[2] = metric_part(mate)
    c_b = send(part.at[2], rb, tail_ssem.at[3], tail_rsem.at[3], (b, mate))

    total = d1[y]
    for i in (1, 2, 3):
        yy, dev = y_peer(i)
        remote(d1.at[yy], dry.at[yy], y_ssem.at[i], y_rsem.at[yy], dev).wait_recv()
        total = total + dry[yy]
    for zz in range(8):
        d2[zz] = total[:, zz * 8 : zz * 8 + 8, :]
    for i in range(1, 8):
        zz, dev = z_peer(i)
        send(d2.at[zz], drz.at[z], z_ssem.at[i], z_rsem.at[z], dev)

    mine = metric_part(s)

    total = d2[z]
    for i in range(1, 8):
        zz, dev = z_peer(i)
        remote(d2.at[zz], drz.at[zz], z_ssem.at[i], z_rsem.at[zz], dev).wait_recv()
        total = total + drz[zz]
    d3[...] = total
    here = x_hi * 2 + x_lo
    for i in (1, 2, 3):
        xx, dev = x_peer(i)
        send(d3.at[xx % 2], drx.at[here], x_ssem.at[i], x_rsem.at[here], dev)
    drx[here] = d3[x_lo]

    c_b.wait_recv()
    part[3] = mine + rb[...]

    for i in (1, 2, 3):
        xx, dev = x_peer(i)
        remote(d3.at[0], drx.at[xx], x_ssem.at[i], x_rsem.at[xx], dev).wait_recv()
    d4[...] = (drx[0] + drx[1]) + (drx[2] + drx[3])
    c_4 = send(d4, dr4, tail_ssem.at[4], tail_rsem.at[4], (b, mate))
    c_4.wait_recv()

    @pl.when(core == 0)
    def _():
        dens_out_ref[:, pl.ds(0, QW)] = d4[...]
        dens_out_ref[:, pl.ds(QW, QW)] = dr4[...]

    @pl.when(core == 1)
    def _():
        dens_out_ref[:, pl.ds(0, QW)] = dr4[...]
        dens_out_ref[:, pl.ds(QW, QW)] = d4[...]

    c_x.wait_recv()
    gamma_ref[...] = (part[3] + rx[...]).T

    for c in firsts:
        c.wait_send()

    def drain(k, carry):
        for q in range(4):
            hop(k - 1, k, q).wait_send()
        return carry

    lax.fori_loop(1, STEPS, drain, 0)
    for c in sends:
        c.wait_send()


def per_device(factors, occ_energy, vir_energy, metric):
    vmem = pl.BlockSpec(memory_space=pltpu.VMEM)
    dma = pltpu.SemaphoreType.DMA
    gamma, density = pl.pallas_call(
        kernel,
        out_shape=(
            jax.ShapeDtypeStruct((QW, V), F32),
            jax.ShapeDtypeStruct((8, V), F32),
        ),
        in_specs=[
            pl.BlockSpec(memory_space=pltpu.SMEM),
            vmem,
            vmem,
            pl.BlockSpec(memory_space=pl.ANY),
        ],
        out_specs=(vmem, vmem),
        scratch_shapes=[
            pltpu.VMEM((9, 4, V, QW), BF16),
            pltpu.VMEM((4, V, QW), F32),
            pltpu.VMEM((2, V, QW), F32),
            pltpu.VMEM((V, V), F32),
            pltpu.VMEM((V, V), F32),
            pltpu.VMEM((V, V), BF16),
            pltpu.VMEM((4 * QW, 4 * QW), F32),
            pltpu.VMEM((4 * QW, 4 * QW), BF16),
            pltpu.VMEM((4 * QW, 4 * QW), BF16),
            pltpu.VMEM((4, V, QW), BF16),
            pltpu.VMEM((4, V, QW), BF16),
            pltpu.VMEM((4, V, QW), F32),
            pltpu.VMEM((V, QW), F32),
            pltpu.VMEM((V, QW), F32),
            pltpu.VMEM((V, QW), F32),
            pltpu.VMEM((V, QW), F32),
            pltpu.VMEM((4, 2, 64, QW), F32),
            pltpu.VMEM((4, 2, 64, QW), F32),
            pltpu.VMEM((8, 2, 8, QW), F32),
            pltpu.VMEM((8, 2, 8, QW), F32),
            pltpu.VMEM((2, 8, QW), F32),
            pltpu.VMEM((4, 8, QW), F32),
            pltpu.VMEM((8, QW), F32),
            pltpu.VMEM((8, QW), F32),
            dma((2,)),
            dma((5,)),
            dma((9, 4)),
            dma((9, 4)),
            dma((5,)),
            dma((5,)),
            dma((4,)),
            dma((4,)),
            dma((8,)),
            dma((8,)),
            dma((4,)),
            dma((4,)),
        ],
        compiler_params=pltpu.CompilerParams(
            collective_id=0, has_side_effects=True, vmem_limit_bytes=60 * 1024 * 1024
        ),
    )(occ_energy, factors, vir_energy.reshape(1, V), metric)
    return gamma.reshape(QW, 1, V), density


def solution(mesh):
    return jax.shard_map(
        per_device,
        mesh=mesh,
        in_specs=(P("blk", None, "sec"), P(), P(), P()),
        out_specs=(P("sec", "blk", None), P("blk", None)),
        check_vma=False,
    )
```

time: 951 us -> 217 us (0.23)
  waiting for transfers between devices: 771 us -> 0 us
  Pallas kernels: 0 us -> 211 us
  starting transfers between devices: 60.1 us -> 0 us
  matrix products: 45.1 us -> 0 us
  blocking collectives: 21.7 us -> 0 us
  between operations: 19.1 us -> 0.64 us
  local copies, waits for them, and re-layouts: 21.6 us -> 3.7 us
  other arithmetic: 11.2 us -> 0 us
    ppermute x13 -> x0, waiting for transfers between devices: 511 us -> none  [from_behind(): lax.ppermute(shard, axis, [(i, (i + by) % devices) for i in range(devices)])]
    pallas_call x0 -> x1, Pallas kernels: none -> 211 us  [per_device(): pl.pallas_call(kernel, out_shape=(jax.ShapeDtypeStruct((QW, V), F32), jax...]
    psum x1 -> x0, waiting for transfers between devices: 199 us -> none  [per_device(): density_all = lax.psum(density, ('blk', 'sec'))]
    ppermute x13 -> x0, starting transfers between devices: 56 us -> none  [from_behind(): lax.ppermute(shard, axis, [(i, (i + by) % devices) for i in range(devices)])]
    dot_general x22 -> x0, matrix products: 45.1 us -> none  [the longest x4 8.98 us: one_pair(): lax.dot_general(left_block, right_block, (((1,), (1,)), ((), ())), prefer...]
    reduce_scatter x1 -> x0, waiting for transfers between devices: 44.9 us -> none  [per_device(): lax.psum_scatter(own_term + jnp.einsum('pq,ipa->qia', metric_rows, carrie...]
    all_to_all x1 -> x0, blocking collectives: 21.7 us -> none  [per_device(): lax.all_to_all(jnp.stack(segmented, 0), 'sec', split_axis=0, concat_axis=...]
    all_to_all x1 -> x0, waiting for transfers between devices: 16.1 us -> none  [per_device(): lax.all_to_all(acc_part[None], 'sec', split_axis=2, concat_axis=0, tiled=...]
  transfers between devices with their start and end apart: 17 -> 0, of which waited for: 16 -> 0; matrix products, arithmetic and copies ran while one was open for 5% -> 0% of each run, Pallas kernels for 0% -> 0%
where the time goes in v1:
time: 217 us; the launch traced here: 216 us
  Pallas kernels  211 us (97%)
  local copies, waits for them, and re-layouts  3.7 us (2%)
    pallas_call x1, Pallas kernels, per_device(): pl.pallas_call(kernel, out_shape=(jax.ShapeDtypeStruct((QW, V), F32), jax...  211 us

profile of v1, /device:TPU:1, one launch (start us, length us, event | category | flops | bytes accessed | tf_op | source)
XLA Modules:
  0.0 215.8 jit_solution(14514376367909366634)
XLA Ops:
  0.6 211.5 %shard_map.59 = (f32[256,512]{1,0:T(8,128)}, f32[8,512]{1,0:T(8,128)}) custom-call(f32[64]{0:T(128)} %occ_ref.1, bf16[1,512,256]{2,1,0:T(8,128)(2,1)} %f_ref.1, f32[1,512]{1,0:T(1,128)} %bitcast.3, f32[1024,1024]{1,0:T(8,128)} %metric_ref.1), custom_call_target="tpu_custom_call" | custom-call | tf_op jit(solution)/shard_map/pallas_call | solution.py:340
  212.1 2.4 %copy.6 = f32[256,1,512]{2,1,0:T(1,128)} copy(f32[256,1,512]{2,0,1:T(8,128)} %bitcast.2) | data formatting | bytes 1048576
  214.5 1.3 copy.8

commit v2 on v1

--- a/solution.py
+++ b/solution.py
@@ -14,7 +14,6 @@
 V = 512
 QW = 256
 NB = 64
-STEPS = 8
 ROWS = 256
 
 
@@ -29,7 +28,8 @@
     metric_ref,
     gamma_ref,
     dens_out_ref,
-    slots,
+    jb,
+    rbuf,
     g_acc,
     dens,
     vir_sum,
@@ -55,8 +55,12 @@
     dr4,
     local_sem,
     init_ssem,
-    ssem,
+    zinit_ssem,
+    z_fwd,
+    zr_fwd,
+    y_fwd,
     rsem,
+    rrsem,
     tail_ssem,
     tail_rsem,
     y_ssem,
@@ -73,57 +77,49 @@
     x_lo = b // 32
     y = (b // 8) % 4
     z = b % 8
-    far = s // 2
     mate = s + 1 - 2 * core
     across = (s + 2) % 4
     diag = 3 - s
-    sign = 1 - 2 * core
-    nxt = (b + sign + NB) % NB
-    prv = (b - sign + NB) % NB
 
     def y_peer(i):
         yy = (y + i) % 4
         return yy, (x_lo * 32 + yy * 8 + z, s)
 
     def z_peer(i):
-        zz = (z + i) % 8
+        zz = (z + i + 8) % 8
         return zz, (x_lo * 32 + y * 8 + zz, s)
 
     def x_peer(i):
         xx = (x_hi * 2 + x_lo + i) % 4
         return xx, ((xx % 2) * 32 + y * 8 + z, (xx // 2) * 2 + core)
 
+    def row_peer(rows, sec):
+        return ((b + 8 * rows + NB) % NB, sec)
+
     barrier = pltpu.get_barrier_semaphore()
 
     def greet(dev):
         pl.semaphore_signal(barrier, inc=1, device_id=dev, device_id_type=MESH)
 
-    for t in (mate, across, diag):
-        greet((b, t))
-    greet((nxt, s))
-    greet((prv, s))
-    greet(((b + 8) % NB, 2))
-    greet(((b + NB - 8) % NB, 3))
-
-    @pl.when(far == 1)
-    def _():
-        source = (b - 8 * sign + NB) % NB
-        for t in range(4):
-            greet((source, t))
-
+    greet((b, mate))
+    for i in (1, 2, 3):
+        greet(x_peer(i)[1])
+    for c in range(2):
+        greet(row_peer(1 + x_hi, x_hi * 2 + c))
+        greet(row_peer(-1 - x_hi, x_hi * 2 + c))
     for i in (1, 2, 3):
         greet(y_peer(i)[1])
     for i in range(1, 8):
         greet(z_peer(i)[1])
-    for i in (1, 3):
-        greet(x_peer(i)[1])
 
     metric_copy = pltpu.make_async_copy(metric_ref, m_f32, local_sem.at[1])
     metric_copy.start()
-    own_copy = pltpu.make_async_copy(f_ref.at[0], slots.at[0, s], local_sem.at[0])
+    own_copy = pltpu.make_async_copy(f_ref.at[0], jb.at[8, s], local_sem.at[0])
     own_copy.start()
-
-    pl.semaphore_wait(barrier, 19 + 4 * far)
+    vir_rows = jnp.broadcast_to(vir_ref[...], (V, V))
+    vir_sum[...] = vir_rows + vir_rows.T
+
+    pl.semaphore_wait(barrier, 18)
 
     def remote(src, dst, send, recv, dev):
         return pltpu.make_async_remote_copy(
@@ -131,72 +127,185 @@
             device_id=dev, device_id_type=MESH,
         )
 
-    firsts = []
-    for i, (dev, entry) in enumerate(
-        (
-            ((b, across), 0),
-            ((b, mate), 0),
-            ((b, diag), 0),
-            (((b + 8) % NB, 2), 8),
-            (((b + NB - 8) % NB, 3), 8),
-        )
-    ):
-        c = remote(f_ref.at[0], slots.at[entry, s], init_ssem.at[i], rsem.at[entry, s], dev)
-        c.start()
-        firsts.append(c)
-
-    def hop(src_entry, dst_entry, q):
-        return remote(
-            slots.at[src_entry, q], slots.at[dst_entry, q],
-            ssem.at[dst_entry, q], rsem.at[dst_entry, q], (nxt, s),
-        )
-
     def arrived(entry, q):
         remote(
-            slots.at[entry, q], slots.at[entry, q],
-            ssem.at[entry, q], rsem.at[entry, q], (nxt, s),
+            jb.at[entry, q], jb.at[entry, q], z_fwd.at[0, 0], rsem.at[entry, q], (b, mate)
         ).wait_recv()
 
-    order = (s, mate, across, diag)
+    def slot_of(p):
+        return (z + ((p + 1) // 2) * (1 - 2 * (p % 2)) + 8) % 8
+
+    def first(i, src, dst, recv, dev):
+        return remote(src, dst, init_ssem.at[i], recv, dev)
+
+    def first_across():
+        return first(0, f_ref.at[0], jb.at[8, s], rsem.at[8, s], (b, across))
+
+    def first_mate():
+        return first(1, f_ref.at[0], jb.at[8, s], rsem.at[8, s], (b, mate))
+
+    def first_up():
+        return first(2, f_ref.at[0], jb.at[z, s], rsem.at[z, s], row_peer(1, 0))
+
+    def first_down():
+        return first(3, f_ref.at[0], jb.at[z, s], rsem.at[z, s], row_peer(-1, 1))
+
+    def chain_up():
+        return first(2, f_ref.at[0], rbuf.at[1], rrsem.at[1], row_peer(2, 3))
+
+    def chain_down():
+        return first(3, f_ref.at[0], rbuf.at[0], rrsem.at[0], row_peer(-2, 3))
+
+    def pass_on():
+        return first(4, jb.at[8, across], jb.at[8, across], rsem.at[8, across], (b, mate))
+
+    def ring_start(item, way, src, q):
+        return remote(
+            src, jb.at[z, q], zinit_ssem.at[item, way], rsem.at[z, q], z_peer(2 * way - 1)[1]
+        )
+
+    def ring_start_r(way):
+        return remote(
+            jb.at[8, across], rbuf.at[z], zinit_ssem.at[2, way], rrsem.at[z],
+            z_peer(2 * way - 1)[1],
+        )
+
+    def chain_start(way):
+        return remote(
+            rbuf.at[1 - way], jb.at[z, 3], zinit_ssem.at[3, way], rsem.at[z, 3],
+            z_peer(2 * way - 1)[1],
+        )
+
+    def ring_hop(slot, q, way):
+        return remote(
+            jb.at[slot, q], jb.at[slot, q], z_fwd.at[slot, q], rsem.at[slot, q],
+            z_peer(2 * way - 1)[1],
+        )
+
+    def ring_hop_r(slot, way):
+        return remote(
+            rbuf.at[slot], rbuf.at[slot], zr_fwd.at[slot], rrsem.at[slot],
+            z_peer(2 * way - 1)[1],
+        )
+
+    def to_rows(slot, src):
+        return (
+            remote(src, jb.at[slot, across], y_fwd.at[slot, 0], rsem.at[slot, across], row_peer(1, 0)),
+            remote(src, jb.at[slot, across], y_fwd.at[slot, 1], rsem.at[slot, across], row_peer(-1, 1)),
+        )
+
+    def to_far_row(slot, q):
+        up = jnp.where(slot > z, 2, -2)
+        return remote(
+            jb.at[slot, q], jb.at[slot, q], y_fwd.at[slot, q], rsem.at[slot, q], row_peer(up, 3)
+        )
+
+    def goes_on(p, left4):
+        d = (p + 1) // 2
+        return (d < 3) | ((d == 3) & (p % 2 == left4))
+
+    first_across().start()
+    first_mate().start()
+
+    @pl.when(x_hi == 0)
+    def _():
+        first_up().start()
+        first_down().start()
+
+    @pl.when(s == 2)
+    def _():
+        for way in (1, 0):
+            ring_start(2, way, f_ref.at[0], 2).start()
+
+    @pl.when(s == 3)
+    def _():
+        chain_up().start()
+        chain_down().start()
 
     own_copy.wait()
-
-    @pl.when(far == 0)
-    def _():
-        for n, q in enumerate(order):
-            if n > 0:
-                arrived(0, q)
-            hop(0, 1, q).start()
-
-    @pl.when(far == 1)
-    def _():
-        for q in order:
-            arrived(8, q)
-            hop(8, 1, q).start()
-        for q in order[1:]:
-            arrived(0, q)
-
-    vir_rows = jnp.broadcast_to(vir_ref[...], (V, V))
-    vir_sum[...] = vir_rows + vir_rows.T
+    arrived(8, across)
+    pass_on().start()
+
+    @pl.when(x_hi == 0)
+    def _():
+        for way in (1, 0):
+            ring_start_r(way).start()
+        for c in to_rows(z, jb.at[8, across]):
+            c.start()
+        for q in range(2):
+            arrived(z, q)
+            for way in (1, 0):
+                ring_start(q, way, jb.at[z, q], q).start()
+
+    @pl.when(s == 2)
+    def _():
+        for way in (1, 0):
+            ring_start(0, way, jb.at[8, 0], 0).start()
+
+    @pl.when(s == 3)
+    def _():
+        for way in (1, 0):
+            remote(
+                rbuf.at[0], rbuf.at[1 - way], z_fwd.at[0, 0], rrsem.at[1 - way], (b, mate)
+            ).wait_recv()
+
+        @pl.when(z < 7)
+        def _():
+            chain_start(1).start()
+
+        @pl.when(z > 0)
+        def _():
+            chain_start(0).start()
+
+    arrived(8, mate)
+
+    @pl.when(s == 2)
+    def _():
+        for way in (1, 0):
+            ring_start(3, way, jb.at[8, 3], 3).start()
+
+    arrived(8, diag)
+
+    @pl.when(s == 2)
+    def _():
+        for way in (1, 0):
+            ring_start(1, way, jb.at[8, 1], 1).start()
+
     g_acc[...] = jnp.zeros_like(g_acc)
     dens[...] = jnp.zeros_like(dens)
-    metric_copy.wait()
-    for i in range(4):
-        rows = pl.ds(i * QW, QW)
-        m = m_f32[rows, :]
-        hi = m.astype(BF16)
-        m_hi[rows, :] = hi
-        m_lo[rows, :] = (m - hi.astype(F32)).astype(BF16)
+
+    @pl.when(s == 3)
+    def _():
+        def chain(t, carry):
+            @pl.when(z - t >= 0)
+            def _():
+                arrived(z - t, 3)
+
+                @pl.when(z < 7)
+                def _():
+                    ring_hop(z - t, 3, 1).start()
+
+            @pl.when(z + t < 8)
+            def _():
+                arrived(z + t, 3)
+
+                @pl.when(z > 0)
+                def _():
+                    ring_hop(z + t, 3, 0).start()
+
+            return carry
+
+        lax.fori_loop(1, 8, chain, 0)
 
     own_e = occ_ref[b]
 
-    def pair(entry, offset):
-        e_sum = own_e + occ_ref[(b - sign * offset + 2 * NB) % NB]
+    def pair(entry, other):
+        e_sum = own_e + occ_ref[other]
         for rc in range(V // ROWS):
             rows = pl.ds(rc * ROWS, ROWS)
-            acc = dot(slots[0, 0, rows, :], slots[entry, 0], NT)
+            acc = dot(jb[8, 0, rows, :], jb[entry, 0], NT)
             for q in range(1, 4):
-                acc = acc + dot(slots[0, q, rows, :], slots[entry, q], NT)
+                acc = acc + dot(jb[8, q, rows, :], jb[entry, q], NT)
             t = acc / (e_sum - vir_sum[rows, :])
             t_buf[rows, :] = t
             tb_buf[rows, :] = t.astype(BF16)
@@ -204,26 +313,75 @@
             rows = pl.ds(rc * ROWS, ROWS)
             ub = (2.0 * t_buf[rows, :] - t_buf[:, rows].T).astype(BF16)
             for q in range(4):
-                g_acc[q, rows, :] += dot(ub, slots[entry, q], NN)
+                g_acc[q, rows, :] += dot(ub, jb[entry, q], NN)
             for h in range(2):
                 dens[h, rows, :] += dot(ub, tb_buf[pl.ds(h * QW, QW), :], NT)
 
-    @pl.when(s != 1)
-    def _():
-        pair(8 * far, 8 * far)
-
-    def step(k, carry):
-        for q in order:
-            arrived(k, q)
-
-            @pl.when(k < STEPS - 1)
+    def relay(p, q, left4):
+        slot = slot_of(p)
+        arrived(slot, q)
+
+        @pl.when(goes_on(p, left4))
+        def _():
+            ring_hop(slot, q, p % 2).start()
+
+    def place(p, carry):
+        slot = slot_of(p)
+
+        @pl.when((p < 7) & (x_hi == 0))
+        def _():
+            nslot = slot_of(p + 1)
+            remote(
+                rbuf.at[0], rbuf.at[nslot], zr_fwd.at[0], rrsem.at[nslot], (b, mate)
+            ).wait_recv()
+
+            @pl.when(goes_on(p + 1, 1 - core))
             def _():
-                hop(k, k + 1, q).start()
-
-        pair(k, k + 8 * far)
+                ring_hop_r(nslot, (p + 1) % 2).start()
+
+            for c in to_rows(nslot, rbuf.at[nslot]):
+                c.start()
+            relay(p + 1, 0, 1)
+            relay(p + 1, 1, 0)
+
+        @pl.when((p < 7) & (s == 2))
+        def _():
+            for q, left4 in ((2, 0), (0, 1), (3, 0), (1, 1)):
+                relay(p + 1, q, left4)
+                if q < 3:
+                    to_far_row(slot_of(p + 1), q).start()
+
+        @pl.when(x_hi == 0)
+        def _():
+            arrived(slot, 2)
+            arrived(slot, 3)
+
+        @pl.when((p > 0) & (s == 3))
+        def _():
+            for q in range(3):
+                arrived(slot, q)
+
+        shift = jnp.where(s == 0, -1, jnp.where(s == 1, 1, 0))
+        shift = jnp.where(s == 3, jnp.where(slot > z, -2, 2), shift)
+        other = ((b // 8 + shift + 8) % 8) * 8 + slot
+
+        @pl.when((p > 0) | (s != 3))
+        def _():
+            pair(jnp.where((p == 0) & (s == 2), 8, slot), other)
+
+        @pl.when(p == 0)
+        def _():
+            metric_copy.wait()
+            for i in range(4):
+                rows = pl.ds(i * QW, QW)
+                m = m_f32[rows, :]
+                hi = m.astype(BF16)
+                m_hi[rows, :] = hi
+                m_lo[rows, :] = (m - hi.astype(F32)).astype(BF16)
+
         return carry
 
-    lax.fori_loop(1, STEPS, step, 0)
+    lax.fori_loop(0, 8, place, 0)
 
     sends = []
 
@@ -321,15 +479,76 @@
     c_x.wait_recv()
     gamma_ref[...] = (part[3] + rx[...]).T
 
-    for c in firsts:
-        c.wait_send()
-
-    def drain(k, carry):
-        for q in range(4):
-            hop(k - 1, k, q).wait_send()
+    first_across().wait_send()
+    first_mate().wait_send()
+    pass_on().wait_send()
+
+    @pl.when(x_hi == 0)
+    def _():
+        first_up().wait_send()
+        first_down().wait_send()
+        for way in (1, 0):
+            ring_start_r(way).wait_send()
+            for q in range(2):
+                ring_start(q, way, jb.at[z, q], q).wait_send()
+        for c in to_rows(z, jb.at[8, across]):
+            c.wait_send()
+
+    @pl.when(s == 2)
+    def _():
+        for way in (1, 0):
+            for q in range(4):
+                ring_start(q, way, jb.at[8, q], q).wait_send()
+
+    @pl.when(s == 3)
+    def _():
+        chain_up().wait_send()
+        chain_down().wait_send()
+
+        @pl.when(z < 7)
+        def _():
+            chain_start(1).wait_send()
+
+        @pl.when(z > 0)
+        def _():
+            chain_start(0).wait_send()
+
+    def drain(p, carry):
+        slot = slot_of(p)
+
+        @pl.when(x_hi == 0)
+        def _():
+            for c in to_rows(slot, rbuf.at[slot]):
+                c.wait_send()
+
+            @pl.when(goes_on(p, 1 - core))
+            def _():
+                ring_hop_r(slot, p % 2).wait_send()
+
+            for q, left4 in ((0, 1), (1, 0)):
+
+                @pl.when(goes_on(p, left4))
+                def _():
+                    ring_hop(slot, q, p % 2).wait_send()
+
+        @pl.when(s == 2)
+        def _():
+            for q, left4 in ((2, 0), (0, 1), (3, 0), (1, 1)):
+
+                @pl.when(goes_on(p, left4))
+                def _():
+                    ring_hop(slot, q, p % 2).wait_send()
+
+                if q < 3:
+                    to_far_row(slot, q).wait_send()
+
+        @pl.when((s == 3) & (((slot < z) & (z < 7)) | ((slot > z) & (z > 0))))
+        def _():
+            ring_hop(slot, 3, 0).wait_send()
+
         return carry
 
-    lax.fori_loop(1, STEPS, drain, 0)
+    lax.fori_loop(1, 8, drain, 0)
     for c in sends:
         c.wait_send()
 
@@ -352,6 +571,7 @@
         out_specs=(vmem, vmem),
         scratch_shapes=[
             pltpu.VMEM((9, 4, V, QW), BF16),
+            pltpu.VMEM((8, V, QW), BF16),
             pltpu.VMEM((4, V, QW), F32),
             pltpu.VMEM((2, V, QW), F32),
             pltpu.VMEM((V, V), F32),
@@ -377,8 +597,12 @@
             pltpu.VMEM((8, QW), F32),
             dma((2,)),
             dma((5,)),
+            dma((4, 2)),
+            dma((8, 4)),
+            dma((8,)),
+            dma((8, 4)),
             dma((9, 4)),
-            dma((9, 4)),
+            dma((8,)),
             dma((5,)),
             dma((5,)),
             dma((4,)),

time: 217 us -> 127 us (0.59)
  Pallas kernels: 211 us -> 123 us
    pallas_call x1, Pallas kernels: 211 us -> 123 us  [per_device(): pl.pallas_call(kernel, out_shape=(jax.ShapeDtypeStruct((QW, V), F32), jax...]
where the time goes in v2:
time: 127 us
  Pallas kernels  123 us (97%)
  local copies, waits for them, and re-layouts  3.7 us (3%)
    pallas_call x1, Pallas kernels, per_device(): pl.pallas_call(kernel, out_shape=(jax.ShapeDtypeStruct((QW, V), F32), jax...  123 us
    unnamed x2, local copies, waits for them, and re-layouts  3.7 us

profile of v2, /device:TPU:1, one launch (start us, length us, event | category | flops | bytes accessed | tf_op | source)
XLA Modules:
  0.0 127.3 jit_solution(2423370558994167792)
XLA Ops:
  0.6 122.9 %shard_map.59 = (f32[256,512]{1,0:T(8,128)}, f32[8,512]{1,0:T(8,128)}) custom-call(f32[64]{0:T(128)} %occ_ref.1, bf16[1,512,256]{2,1,0:T(8,128)(2,1)} %f_ref.1, f32[1,512]{1,0:T(1,128)} %bitcast.3, f32[1024,1024]{1,0:T(8,128)} %metric_ref.1), custom_call_target="tpu_custom_call" | custom-call | tf_op jit(solution)/shard_map/pallas_call | solution.py:559
  123.6 2.4 %copy.6 = f32[256,1,512]{2,1,0:T(1,128)} copy(f32[256,1,512]{2,0,1:T(8,128)} %bitcast.2) | data formatting | bytes 1048576
  126.0 1.3 %copy.8 = f32[8,512]{1,0:T(8,128)} copy(f32[8,512]{1,0:T(8,128)} %get-tuple-element.11) | data formatting | bytes 32768

commit v3 on v2

--- a/solution.py
+++ b/solution.py
@@ -51,8 +51,8 @@
     drz,
     d3,
     drx,
-    d4,
-    dr4,
+    occ_sm,
+    vir_vm,
     local_sem,
     init_ssem,
     zinit_ssem,
@@ -63,6 +63,8 @@
     rrsem,
     tail_ssem,
     tail_rsem,
+    half_ssem,
+    half_rsem,
     y_ssem,
     y_rsem,
     z_ssem,
@@ -89,9 +91,9 @@
         zz = (z + i + 8) % 8
         return zz, (x_lo * 32 + y * 8 + zz, s)
 
-    def x_peer(i):
+    def x_peer(i, to_core):
         xx = (x_hi * 2 + x_lo + i) % 4
-        return xx, ((xx % 2) * 32 + y * 8 + z, (xx // 2) * 2 + core)
+        return xx, ((xx % 2) * 32 + y * 8 + z, (xx // 2) * 2 + to_core)
 
     def row_peer(rows, sec):
         return ((b + 8 * rows + NB) % NB, sec)
@@ -101,9 +103,15 @@
     def greet(dev):
         pl.semaphore_signal(barrier, inc=1, device_id=dev, device_id_type=MESH)
 
+    occ_copy = pltpu.make_async_copy(occ_ref, occ_sm, local_sem.at[2])
+    vir_copy = pltpu.make_async_copy(vir_ref, vir_vm, local_sem.at[3])
+    metric_copy = pltpu.make_async_copy(metric_ref, m_f32, local_sem.at[1])
+    own_copy = pltpu.make_async_copy(f_ref.at[0], jb.at[8, s], local_sem.at[0])
+
     greet((b, mate))
     for i in (1, 2, 3):
-        greet(x_peer(i)[1])
+        for c in range(2):
+            greet(x_peer(i, c)[1])
     for c in range(2):
         greet(row_peer(1 + x_hi, x_hi * 2 + c))
         greet(row_peer(-1 - x_hi, x_hi * 2 + c))
@@ -112,14 +120,17 @@
     for i in range(1, 8):
         greet(z_peer(i)[1])
 
-    metric_copy = pltpu.make_async_copy(metric_ref, m_f32, local_sem.at[1])
+    vir_copy.start()
+    occ_copy.start()
+    own_copy.start()
     metric_copy.start()
-    own_copy = pltpu.make_async_copy(f_ref.at[0], jb.at[8, s], local_sem.at[0])
-    own_copy.start()
-    vir_rows = jnp.broadcast_to(vir_ref[...], (V, V))
+    vir_copy.wait()
+    vir_rows = jnp.broadcast_to(vir_vm[...], (V, V))
     vir_sum[...] = vir_rows + vir_rows.T
-
-    pl.semaphore_wait(barrier, 18)
+    g_acc[...] = jnp.zeros_like(g_acc)
+    dens[...] = jnp.zeros_like(dens)
+
+    pl.semaphore_wait(barrier, 21)
 
     def remote(src, dst, send, recv, dev):
         return pltpu.make_async_remote_copy(
@@ -145,10 +156,14 @@
         return first(1, f_ref.at[0], jb.at[8, s], rsem.at[8, s], (b, mate))
 
     def first_up():
-        return first(2, f_ref.at[0], jb.at[z, s], rsem.at[z, s], row_peer(1, 0))
+        return first(
+            2, jb.at[8, across], jb.at[z, across], rsem.at[z, across], row_peer(1, 0)
+        )
 
     def first_down():
-        return first(3, f_ref.at[0], jb.at[z, s], rsem.at[z, s], row_peer(-1, 1))
+        return first(
+            3, jb.at[8, across], jb.at[z, across], rsem.at[z, across], row_peer(-1, 1)
+        )
 
     def chain_up():
         return first(2, f_ref.at[0], rbuf.at[1], rrsem.at[1], row_peer(2, 3))
@@ -166,8 +181,7 @@
 
     def ring_start_r(way):
         return remote(
-            jb.at[8, across], rbuf.at[z], zinit_ssem.at[2, way], rrsem.at[z],
-            z_peer(2 * way - 1)[1],
+            f_ref.at[0], rbuf.at[z], zinit_ssem.at[0, way], rrsem.at[z], z_peer(2 * way - 1)[1]
         )
 
     def chain_start(way):
@@ -190,8 +204,8 @@
 
     def to_rows(slot, src):
         return (
-            remote(src, jb.at[slot, across], y_fwd.at[slot, 0], rsem.at[slot, across], row_peer(1, 0)),
-            remote(src, jb.at[slot, across], y_fwd.at[slot, 1], rsem.at[slot, across], row_peer(-1, 1)),
+            remote(src, jb.at[slot, s], y_fwd.at[slot, 0], rsem.at[slot, s], row_peer(1, 0)),
+            remote(src, jb.at[slot, s], y_fwd.at[slot, 1], rsem.at[slot, s], row_peer(-1, 1)),
         )
 
     def to_far_row(slot, q):
@@ -204,43 +218,96 @@
         d = (p + 1) // 2
         return (d < 3) | ((d == 3) & (p % 2 == left4))
 
+    def relay(p, q, left4):
+        slot = slot_of(p)
+        arrived(slot, q)
+
+        @pl.when(goes_on(p, left4))
+        def _():
+            ring_hop(slot, q, p % 2).start()
+
+    def relay_r(p):
+        slot = slot_of(p)
+        remote(
+            rbuf.at[0], rbuf.at[slot], zr_fwd.at[0], rrsem.at[slot], (b, mate)
+        ).wait_recv()
+
+        @pl.when(goes_on(p, 1 - core))
+        def _():
+            ring_hop_r(slot, p % 2).start()
+
+        for c in to_rows(slot, rbuf.at[slot]):
+            c.start()
+
+    @pl.when(s == 2)
+    def _():
+        for way in (1, 0):
+            ring_start(2, way, f_ref.at[0], 2).start()
+
+    @pl.when(x_hi == 0)
+    def _():
+        for way in (1, 0):
+            ring_start_r(way).start()
+
     first_across().start()
     first_mate().start()
 
     @pl.when(x_hi == 0)
     def _():
+        for c in to_rows(z, f_ref.at[0]):
+            c.start()
+
+    @pl.when(s == 3)
+    def _():
+        chain_up().start()
+        chain_down().start()
+
+    occ_copy.wait()
+    own_copy.wait()
+    metric_copy.wait()
+    for i in range(4):
+        rows = pl.ds(i * QW, QW)
+        m = m_f32[rows, :]
+        hi = m.astype(BF16)
+        m_hi[rows, :] = hi
+        m_lo[rows, :] = (m - hi.astype(F32)).astype(BF16)
+
+    arrived(8, mate)
+
+    @pl.when(x_hi == 0)
+    def _():
+        for p in (1, 2):
+            relay_r(p)
+
+    @pl.when(s == 2)
+    def _():
+        for way in (1, 0):
+            ring_start(3, way, jb.at[8, 3], 3).start()
+        for p in (1, 2):
+            relay(p, 2, 0)
+            to_far_row(slot_of(p), 2).start()
+
+    arrived(8, across)
+    pass_on().start()
+
+    @pl.when(x_hi == 0)
+    def _():
         first_up().start()
         first_down().start()
+        for p in (3, 4):
+            relay_r(p)
 
     @pl.when(s == 2)
     def _():
         for way in (1, 0):
-            ring_start(2, way, f_ref.at[0], 2).start()
-
-    @pl.when(s == 3)
-    def _():
-        chain_up().start()
-        chain_down().start()
-
-    own_copy.wait()
-    arrived(8, across)
-    pass_on().start()
-
-    @pl.when(x_hi == 0)
-    def _():
-        for way in (1, 0):
-            ring_start_r(way).start()
-        for c in to_rows(z, jb.at[8, across]):
-            c.start()
-        for q in range(2):
-            arrived(z, q)
-            for way in (1, 0):
-                ring_start(q, way, jb.at[z, q], q).start()
+            ring_start(0, way, jb.at[8, 0], 0).start()
+
+    arrived(8, diag)
 
     @pl.when(s == 2)
     def _():
         for way in (1, 0):
-            ring_start(0, way, jb.at[8, 0], 0).start()
+            ring_start(1, way, jb.at[8, 1], 1).start()
 
     @pl.when(s == 3)
     def _():
@@ -257,25 +324,6 @@
         def _():
             chain_start(0).start()
 
-    arrived(8, mate)
-
-    @pl.when(s == 2)
-    def _():
-        for way in (1, 0):
-            ring_start(3, way, jb.at[8, 3], 3).start()
-
-    arrived(8, diag)
-
-    @pl.when(s == 2)
-    def _():
-        for way in (1, 0):
-            ring_start(1, way, jb.at[8, 1], 1).start()
-
-    g_acc[...] = jnp.zeros_like(g_acc)
-    dens[...] = jnp.zeros_like(dens)
-
-    @pl.when(s == 3)
-    def _():
         def chain(t, carry):
             @pl.when(z - t >= 0)
             def _():
@@ -297,10 +345,10 @@
 
         lax.fori_loop(1, 8, chain, 0)
 
-    own_e = occ_ref[b]
+    own_e = occ_sm[b]
 
     def pair(entry, other):
-        e_sum = own_e + occ_ref[other]
+        e_sum = own_e + occ_sm[other]
         for rc in range(V // ROWS):
             rows = pl.ds(rc * ROWS, ROWS)
             acc = dot(jb[8, 0, rows, :], jb[entry, 0], NT)
@@ -317,48 +365,47 @@
             for h in range(2):
                 dens[h, rows, :] += dot(ub, tb_buf[pl.ds(h * QW, QW), :], NT)
 
-    def relay(p, q, left4):
-        slot = slot_of(p)
-        arrived(slot, q)
-
-        @pl.when(goes_on(p, left4))
-        def _():
-            ring_hop(slot, q, p % 2).start()
-
     def place(p, carry):
         slot = slot_of(p)
 
-        @pl.when((p < 7) & (x_hi == 0))
-        def _():
-            nslot = slot_of(p + 1)
-            remote(
-                rbuf.at[0], rbuf.at[nslot], zr_fwd.at[0], rrsem.at[nslot], (b, mate)
-            ).wait_recv()
-
-            @pl.when(goes_on(p + 1, 1 - core))
-            def _():
-                ring_hop_r(nslot, (p + 1) % 2).start()
-
-            for c in to_rows(nslot, rbuf.at[nslot]):
-                c.start()
-            relay(p + 1, 0, 1)
-            relay(p + 1, 1, 0)
-
-        @pl.when((p < 7) & (s == 2))
-        def _():
-            for q, left4 in ((2, 0), (0, 1), (3, 0), (1, 1)):
-                relay(p + 1, q, left4)
-                if q < 3:
-                    to_far_row(slot_of(p + 1), q).start()
+        @pl.when((p == 0) & (x_hi == 0))
+        def _():
+            for q in (2, 3):
+                arrived(z, q)
+                for way in (1, 0):
+                    ring_start(q, way, jb.at[z, q], q).start()
+            for n in (5, 6):
+                relay_r(n)
+
+        @pl.when((p == 1) & (x_hi == 0))
+        def _():
+            relay_r(7)
+
+        @pl.when((p > 0) & (x_hi == 0))
+        def _():
+            relay(p, 2, 1)
+            relay(p, 3, 0)
+
+        @pl.when((p < 5) & (s == 2))
+        def _():
+            relay(p + 3, 2, 0)
+            to_far_row(slot_of(p + 3), 2).start()
+
+        @pl.when((p > 0) & (s == 2))
+        def _():
+            relay(p, 3, 0)
+            for q in (0, 1):
+                relay(p, q, 1)
+                to_far_row(slot, q).start()
 
         @pl.when(x_hi == 0)
         def _():
-            arrived(slot, 2)
-            arrived(slot, 3)
+            arrived(slot, 0)
+            arrived(slot, 1)
 
         @pl.when((p > 0) & (s == 3))
         def _():
-            for q in range(3):
+            for q in (2, 0, 1):
                 arrived(slot, q)
 
         shift = jnp.where(s == 0, -1, jnp.where(s == 1, 1, 0))
@@ -368,16 +415,6 @@
         @pl.when((p > 0) | (s != 3))
         def _():
             pair(jnp.where((p == 0) & (s == 2), 8, slot), other)
-
-        @pl.when(p == 0)
-        def _():
-            metric_copy.wait()
-            for i in range(4):
-                rows = pl.ds(i * QW, QW)
-                m = m_f32[rows, :]
-                hi = m.astype(BF16)
-                m_hi[rows, :] = hi
-                m_lo[rows, :] = (m - hi.astype(F32)).astype(BF16)
 
         return carry
 
@@ -399,37 +436,51 @@
         g_hi[q] = hi
         g_lo[q] = (g - hi.astype(F32)).astype(BF16)
 
-    def metric_part(t):
+    def metric_part(t, rows):
         cols = pl.ds(pl.multiple_of(t * QW, QW), QW)
         acc = None
         for q in range(4):
-            rows = pl.ds(q * QW, QW)
-            mh = m_hi[rows, cols]
-            ml = m_lo[rows, cols]
-            term = dot(g_hi[q], mh, NN) + (dot(g_lo[q], mh, NN) + dot(g_hi[q], ml, NN))
+            depth = pl.ds(q * QW, QW)
+            mh = m_hi[depth, cols]
+            ml = m_lo[depth, cols]
+            gh = g_hi[q, rows, :]
+            term = dot(gh, mh, NN) + (dot(g_lo[q, rows, :], mh, NN) + dot(gh, ml, NN))
             acc = term if acc is None else acc + term
         return acc
 
-    part[0] = metric_part(diag)
-    c_a = send(part.at[0], ra, tail_ssem.at[1], tail_rsem.at[1], (b, mate))
+    halves = [pl.ds(h * QW, QW) for h in range(2)]
+    everything = pl.ds(0, V)
+    to_mate = []
+    for h, rows in enumerate(halves):
+        part[0, rows, :] = metric_part(diag, rows)
+        to_mate.append(
+            send(
+                part.at[0, rows], ra.at[rows], half_ssem.at[0, h], half_rsem.at[0, h], (b, mate)
+            )
+        )
 
     c_d0.wait_recv()
     for xl in range(2):
         for yy in range(4):
             rows = pl.ds(xl * 256 + yy * 64, 64)
             d1[yy, xl] = dens[core, rows, :] + dr0[rows, :]
-    y_copies = []
     for i in (1, 2, 3):
         yy, dev = y_peer(i)
-        y_copies.append(send(d1.at[yy], dry.at[y], y_ssem.at[i], y_rsem.at[y], dev))
-
-    p_across = metric_part(across)
-    c_a.wait_recv()
-    part[1] = p_across + ra[...]
-    c_x = send(part.at[1], rx, tail_ssem.at[2], tail_rsem.at[2], (b, across))
-
-    part[2] = metric_part(mate)
-    c_b = send(part.at[2], rb, tail_ssem.at[3], tail_rsem.at[3], (b, mate))
+        send(d1.at[yy], dry.at[y], y_ssem.at[i], y_rsem.at[y], dev)
+
+    to_across = []
+    for h, rows in enumerate(halves):
+        p_across = metric_part(across, rows)
+        to_mate[h].wait_recv()
+        part[1, rows, :] = p_across + ra[rows, :]
+        to_across.append(
+            send(
+                part.at[1, rows], rx.at[rows], half_ssem.at[1, h], half_rsem.at[1, h], (b, across)
+            )
+        )
+
+    part[2] = metric_part(mate, everything)
+    c_b = send(part.at[2], rb, tail_ssem.at[1], tail_rsem.at[1], (b, mate))
 
     total = d1[y]
     for i in (1, 2, 3):
@@ -442,7 +493,7 @@
         zz, dev = z_peer(i)
         send(d2.at[zz], drz.at[z], z_ssem.at[i], z_rsem.at[z], dev)
 
-    mine = metric_part(s)
+    part[3] = metric_part(s, everything)
 
     total = d2[z]
     for i in range(1, 8):
@@ -451,33 +502,35 @@
         total = total + drz[zz]
     d3[...] = total
     here = x_hi * 2 + x_lo
+    drx[core, here] = d3[x_lo]
+    send(d3.at[x_lo], drx.at[core, here], tail_ssem.at[2], x_rsem.at[core, here], (b, mate))
     for i in (1, 2, 3):
-        xx, dev = x_peer(i)
-        send(d3.at[xx % 2], drx.at[here], x_ssem.at[i], x_rsem.at[here], dev)
-    drx[here] = d3[x_lo]
+        for c in range(2):
+            xx, dev = x_peer(i, c)
+            send(
+                d3.at[xx % 2], drx.at[core, here], x_ssem.at[c, i], x_rsem.at[core, here], dev
+            )
 
     c_b.wait_recv()
-    part[3] = mine + rb[...]
-
+    part[3] = part[3] + rb[...]
+
+    def dens_arrived(c, xx):
+        remote(
+            d3.at[0], drx.at[c, xx], x_ssem.at[0, 0], x_rsem.at[c, xx], (b, mate)
+        ).wait_recv()
+
+    dens_arrived(1 - core, here)
     for i in (1, 2, 3):
-        xx, dev = x_peer(i)
-        remote(d3.at[0], drx.at[xx], x_ssem.at[i], x_rsem.at[xx], dev).wait_recv()
-    d4[...] = (drx[0] + drx[1]) + (drx[2] + drx[3])
-    c_4 = send(d4, dr4, tail_ssem.at[4], tail_rsem.at[4], (b, mate))
-    c_4.wait_recv()
-
-    @pl.when(core == 0)
-    def _():
-        dens_out_ref[:, pl.ds(0, QW)] = d4[...]
-        dens_out_ref[:, pl.ds(QW, QW)] = dr4[...]
-
-    @pl.when(core == 1)
-    def _():
-        dens_out_ref[:, pl.ds(0, QW)] = dr4[...]
-        dens_out_ref[:, pl.ds(QW, QW)] = d4[...]
-
-    c_x.wait_recv()
-    gamma_ref[...] = (part[3] + rx[...]).T
+        for c in range(2):
+            dens_arrived(c, x_peer(i, c)[0])
+    for c in range(2):
+        dens_out_ref[:, pl.ds(c * QW, QW)] = (drx[c, 0] + drx[c, 1]) + (drx[c, 2] + drx[c, 3])
+
+    for h, rows in enumerate(halves):
+        to_across[h].wait_recv()
+        done = (part[3, rows, :] + rx[rows, :]).T
+        for j in range(2):
+            gamma_ref[pl.ds(2 * h + j, QW, stride=4), :] = done[:, j * 128 : j * 128 + 128]
 
     first_across().wait_send()
     first_mate().wait_send()
@@ -489,9 +542,9 @@
         first_down().wait_send()
         for way in (1, 0):
             ring_start_r(way).wait_send()
-            for q in range(2):
+            for q in (2, 3):
                 ring_start(q, way, jb.at[z, q], q).wait_send()
-        for c in to_rows(z, jb.at[8, across]):
+        for c in to_rows(z, f_ref.at[0]):
             c.wait_send()
 
     @pl.when(s == 2)
@@ -525,7 +578,7 @@
             def _():
                 ring_hop_r(slot, p % 2).wait_send()
 
-            for q, left4 in ((0, 1), (1, 0)):
+            for q, left4 in ((2, 1), (3, 0)):
 
                 @pl.when(goes_on(p, left4))
                 def _():
@@ -553,21 +606,23 @@
         c.wait_send()
 
 
+def hand_over(gamma_ref, dens_ref, gamma_out, dens_out):
+    gamma_out[...] = gamma_ref[...]
+    dens_out[...] = dens_ref[...]
+
+
 def per_device(factors, occ_energy, vir_energy, metric):
     vmem = pl.BlockSpec(memory_space=pltpu.VMEM)
+    hbm = pl.BlockSpec(memory_space=pltpu.HBM)
     dma = pltpu.SemaphoreType.DMA
+    outs = (
+        jax.ShapeDtypeStruct((4 * QW, 128), F32),
+        jax.ShapeDtypeStruct((8, V), F32),
+    )
     gamma, density = pl.pallas_call(
         kernel,
-        out_shape=(
-            jax.ShapeDtypeStruct((QW, V), F32),
-            jax.ShapeDtypeStruct((8, V), F32),
-        ),
-        in_specs=[
-            pl.BlockSpec(memory_space=pltpu.SMEM),
-            vmem,
-            vmem,
-            pl.BlockSpec(memory_space=pl.ANY),
-        ],
+        out_shape=outs,
+        in_specs=[hbm, hbm, hbm, hbm],
         out_specs=(vmem, vmem),
         scratch_shapes=[
             pltpu.VMEM((9, 4, V, QW), BF16),
@@ -592,10 +647,10 @@
             pltpu.VMEM((8, 2, 8, QW), F32),
             pltpu.VMEM((8, 2, 8, QW), F32),
             pltpu.VMEM((2, 8, QW), F32),
-            pltpu.VMEM((4, 8, QW), F32),
-            pltpu.VMEM((8, QW), F32),
-            pltpu.VMEM((8, QW), F32),
-            dma((2,)),
+            pltpu.VMEM((2, 4, 8, QW), F32),
+            pltpu.SMEM((NB,), F32),
+            pltpu.VMEM((1, V), F32),
+            dma((4,)),
             dma((5,)),
             dma((4, 2)),
             dma((8, 4)),
@@ -603,19 +658,28 @@
             dma((8, 4)),
             dma((9, 4)),
             dma((8,)),
-            dma((5,)),
-            dma((5,)),
+            dma((3,)),
+            dma((3,)),
+            dma((2, 2)),
+            dma((2, 2)),
             dma((4,)),
             dma((4,)),
             dma((8,)),
             dma((8,)),
-            dma((4,)),
-            dma((4,)),
+            dma((2, 4)),
+            dma((2, 4)),
         ],
         compiler_params=pltpu.CompilerParams(
             collective_id=0, has_side_effects=True, vmem_limit_bytes=60 * 1024 * 1024
         ),
     )(occ_energy, factors, vir_energy.reshape(1, V), metric)
+    gamma, density = pl.pallas_call(
+        hand_over,
+        out_shape=outs,
+        in_specs=[vmem, vmem],
+        out_specs=(vmem, vmem),
+        compiler_params=pltpu.CompilerParams(vmem_limit_bytes=4 * 1024 * 1024),
+    )(gamma, density)
     return gamma.reshape(QW, 1, V), density
 
 

time: 127 us -> 116 us (0.913)
  Pallas kernels: 123 us -> 113 us
  local copies, waits for them, and re-layouts: 3.7 us -> 1.75 us
    pallas_call x1 -> x2, Pallas kernels: 123 us -> 113 us  [the longest x1 113 us: per_device(): pl.pallas_call(kernel, out_shape=outs, in_specs=[hbm, hbm, hbm, hbm], out...]
    unnamed x2 -> x4, local copies, waits for them, and re-layouts: 3.7 us -> 1.75 us
where the time goes in v3:
time: 116 us
  Pallas kernels  113 us (97%)
  local copies, waits for them, and re-layouts  1.75 us (2%)
    pallas_call x1, Pallas kernels, per_device(): pl.pallas_call(kernel, out_shape=outs, in_specs=[hbm, hbm, hbm, hbm], out...  113 us

profile of v3, /device:TPU:1, one launch (start us, length us, event | category | flops | bytes accessed | tf_op | source)
XLA Modules:
  0.0 115.9 jit_solution(9395270471544745494)
XLA Ops:
  0.6 112.6 %shard_map.59 = (f32[1024,128]{1,0:T(8,128)}, f32[8,512]{1,0:T(8,128)}) custom-call(f32[64]{0:T(128)} %occ_ref.1, bf16[1,512,256]{2,1,0:T(8,128)(2,1)} %f_ref.1, f32[1,512]{1,0:T(1,128)} %bitcast.2, f32[1024,1024]{1,0:T(8,128)} %metric_ref.1), custom_call_target="tpu_custom_call" | custom-call | tf_op jit(solution)/shard_map/pallas_call | solution.py:622
  113.3 0.0 copy-start
  113.3 1.0 copy-done
  114.3 0.0 copy-start.1
  114.3 0.7 copy-done.1
  115.0 0.8 shard_map.60
Async XLA Ops:
  113.3 1.0 copy-start
  114.3 0.7 copy-start.1

commit v4 on v3

--- a/solution.py
+++ b/solution.py
@@ -26,8 +26,7 @@
     f_ref,
     vir_ref,
     metric_ref,
-    gamma_ref,
-    dens_out_ref,
+    out_ref,
     jb,
     rbuf,
     g_acc,
@@ -166,10 +165,10 @@
         )
 
     def chain_up():
-        return first(2, f_ref.at[0], rbuf.at[1], rrsem.at[1], row_peer(2, 3))
+        return first(2, f_ref.at[0], rbuf.at[1], rrsem.at[1, 0], row_peer(2, 3))
 
     def chain_down():
-        return first(3, f_ref.at[0], rbuf.at[0], rrsem.at[0], row_peer(-2, 3))
+        return first(3, f_ref.at[0], rbuf.at[0], rrsem.at[0, 0], row_peer(-2, 3))
 
     def pass_on():
         return first(4, jb.at[8, across], jb.at[8, across], rsem.at[8, across], (b, mate))
@@ -179,9 +178,12 @@
             src, jb.at[z, q], zinit_ssem.at[item, way], rsem.at[z, q], z_peer(2 * way - 1)[1]
         )
 
-    def ring_start_r(way):
+    halves = [pl.ds(h * QW, QW) for h in range(2)]
+
+    def ring_start_r(way, h):
         return remote(
-            f_ref.at[0], rbuf.at[z], zinit_ssem.at[0, way], rrsem.at[z], z_peer(2 * way - 1)[1]
+            f_ref.at[0, halves[h]], rbuf.at[z, halves[h]], zinit_ssem.at[h, way],
+            rrsem.at[z, h], z_peer(2 * way - 1)[1],
         )
 
     def chain_start(way):
@@ -196,10 +198,10 @@
             z_peer(2 * way - 1)[1],
         )
 
-    def ring_hop_r(slot, way):
+    def ring_hop_r(slot, way, h):
         return remote(
-            rbuf.at[slot], rbuf.at[slot], zr_fwd.at[slot], rrsem.at[slot],
-            z_peer(2 * way - 1)[1],
+            rbuf.at[slot, halves[h]], rbuf.at[slot, halves[h]], zr_fwd.at[slot, h],
+            rrsem.at[slot, h], z_peer(2 * way - 1)[1],
         )
 
     def to_rows(slot, src):
@@ -228,14 +230,15 @@
 
     def relay_r(p):
         slot = slot_of(p)
-        remote(
-            rbuf.at[0], rbuf.at[slot], zr_fwd.at[0], rrsem.at[slot], (b, mate)
-        ).wait_recv()
-
-        @pl.when(goes_on(p, 1 - core))
-        def _():
-            ring_hop_r(slot, p % 2).start()
-
+        for h in range(2):
+            ring_hop_r(slot, 0, h).wait_recv()
+
+            @pl.when(goes_on(p, 1 - core))
+            def _():
+                ring_hop_r(slot, p % 2, h).start()
+
+    def rows_r(p):
+        slot = slot_of(p)
         for c in to_rows(slot, rbuf.at[slot]):
             c.start()
 
@@ -246,8 +249,9 @@
 
     @pl.when(x_hi == 0)
     def _():
-        for way in (1, 0):
-            ring_start_r(way).start()
+        for h in range(2):
+            for way in (1, 0):
+                ring_start_r(way, h).start()
 
     first_across().start()
     first_mate().start()
@@ -281,8 +285,6 @@
 
     @pl.when(s == 2)
     def _():
-        for way in (1, 0):
-            ring_start(3, way, jb.at[8, 3], 3).start()
         for p in (1, 2):
             relay(p, 2, 0)
             to_far_row(slot_of(p), 2).start()
@@ -294,8 +296,11 @@
     def _():
         first_up().start()
         first_down().start()
+        for p in (1, 2):
+            rows_r(p)
         for p in (3, 4):
             relay_r(p)
+            rows_r(p)
 
     @pl.when(s == 2)
     def _():
@@ -306,14 +311,15 @@
 
     @pl.when(s == 2)
     def _():
-        for way in (1, 0):
-            ring_start(1, way, jb.at[8, 1], 1).start()
+        for q in (1, 3):
+            for way in (1, 0):
+                ring_start(q, way, jb.at[8, q], q).start()
 
     @pl.when(s == 3)
     def _():
         for way in (1, 0):
             remote(
-                rbuf.at[0], rbuf.at[1 - way], z_fwd.at[0, 0], rrsem.at[1 - way], (b, mate)
+                rbuf.at[0], rbuf.at[1 - way], z_fwd.at[0, 0], rrsem.at[1 - way, 0], (b, mate)
             ).wait_recv()
 
         @pl.when(z < 7)
@@ -360,10 +366,10 @@
         for rc in range(V // ROWS):
             rows = pl.ds(rc * ROWS, ROWS)
             ub = (2.0 * t_buf[rows, :] - t_buf[:, rows].T).astype(BF16)
+            for h in range(2):
+                dens[h, rows, :] += dot(ub, tb_buf[pl.ds(h * QW, QW), :], NT)
             for q in range(4):
                 g_acc[q, rows, :] += dot(ub, jb[entry, q], NN)
-            for h in range(2):
-                dens[h, rows, :] += dot(ub, tb_buf[pl.ds(h * QW, QW), :], NT)
 
     def place(p, carry):
         slot = slot_of(p)
@@ -376,10 +382,12 @@
                     ring_start(q, way, jb.at[z, q], q).start()
             for n in (5, 6):
                 relay_r(n)
+                rows_r(n)
 
         @pl.when((p == 1) & (x_hi == 0))
         def _():
             relay_r(7)
+            rows_r(7)
 
         @pl.when((p > 0) & (x_hi == 0))
         def _():
@@ -391,12 +399,15 @@
             relay(p + 3, 2, 0)
             to_far_row(slot_of(p + 3), 2).start()
 
+        @pl.when((p < 7) & (s == 2))
+        def _():
+            for q in (0, 1):
+                relay(p + 1, q, 1)
+                to_far_row(slot_of(p + 1), q).start()
+
         @pl.when((p > 0) & (s == 2))
         def _():
             relay(p, 3, 0)
-            for q in (0, 1):
-                relay(p, q, 1)
-                to_far_row(slot, q).start()
 
         @pl.when(x_hi == 0)
         def _():
@@ -448,10 +459,11 @@
             acc = term if acc is None else acc + term
         return acc
 
-    halves = [pl.ds(h * QW, QW) for h in range(2)]
     everything = pl.ds(0, V)
     to_mate = []
-    for h, rows in enumerate(halves):
+
+    def first_product(h):
+        rows = halves[h]
         part[0, rows, :] = metric_part(diag, rows)
         to_mate.append(
             send(
@@ -459,14 +471,16 @@
             )
         )
 
+    first_product(0)
     c_d0.wait_recv()
-    for xl in range(2):
-        for yy in range(4):
+    for yy in range(4):
+        for xl in range(2):
             rows = pl.ds(xl * 256 + yy * 64, 64)
             d1[yy, xl] = dens[core, rows, :] + dr0[rows, :]
     for i in (1, 2, 3):
         yy, dev = y_peer(i)
         send(d1.at[yy], dry.at[y], y_ssem.at[i], y_rsem.at[y], dev)
+    first_product(1)
 
     to_across = []
     for h, rows in enumerate(halves):
@@ -524,13 +538,15 @@
         for c in range(2):
             dens_arrived(c, x_peer(i, c)[0])
     for c in range(2):
-        dens_out_ref[:, pl.ds(c * QW, QW)] = (drx[c, 0] + drx[c, 1]) + (drx[c, 2] + drx[c, 3])
+        row_sum = (drx[c, 0] + drx[c, 1]) + (drx[c, 2] + drx[c, 3])
+        for j in range(2):
+            out_ref[pl.ds(4 * QW + (2 * c + j) * 8, 8), :] = row_sum[:, j * 128 : j * 128 + 128]
 
     for h, rows in enumerate(halves):
         to_across[h].wait_recv()
         done = (part[3, rows, :] + rx[rows, :]).T
         for j in range(2):
-            gamma_ref[pl.ds(2 * h + j, QW, stride=4), :] = done[:, j * 128 : j * 128 + 128]
+            out_ref[pl.ds(2 * h + j, QW, stride=4), :] = done[:, j * 128 : j * 128 + 128]
 
     first_across().wait_send()
     first_mate().wait_send()
@@ -541,7 +557,8 @@
         first_up().wait_send()
         first_down().wait_send()
         for way in (1, 0):
-            ring_start_r(way).wait_send()
+            for h in range(2):
+                ring_start_r(way, h).wait_send()
             for q in (2, 3):
                 ring_start(q, way, jb.at[z, q], q).wait_send()
         for c in to_rows(z, f_ref.at[0]):
@@ -576,7 +593,8 @@
 
             @pl.when(goes_on(p, 1 - core))
             def _():
-                ring_hop_r(slot, p % 2).wait_send()
+                for h in range(2):
+                    ring_hop_r(slot, p % 2, h).wait_send()
 
             for q, left4 in ((2, 1), (3, 0)):
 
@@ -606,24 +624,21 @@
         c.wait_send()
 
 
-def hand_over(gamma_ref, dens_ref, gamma_out, dens_out):
-    gamma_out[...] = gamma_ref[...]
-    dens_out[...] = dens_ref[...]
+def hand_over(both_ref, gamma_out, dens_out):
+    gamma_out[...] = both_ref[: 4 * QW, :]
+    for j in range(4):
+        dens_out[:, pl.ds(j * 128, 128)] = both_ref[pl.ds(4 * QW + j * 8, 8), :]
 
 
 def per_device(factors, occ_energy, vir_energy, metric):
     vmem = pl.BlockSpec(memory_space=pltpu.VMEM)
     hbm = pl.BlockSpec(memory_space=pltpu.HBM)
     dma = pltpu.SemaphoreType.DMA
-    outs = (
-        jax.ShapeDtypeStruct((4 * QW, 128), F32),
-        jax.ShapeDtypeStruct((8, V), F32),
-    )
-    gamma, density = pl.pallas_call(
+    both = pl.pallas_call(
         kernel,
-        out_shape=outs,
+        out_shape=jax.ShapeDtypeStruct((4 * QW + 32, 128), F32),
         in_specs=[hbm, hbm, hbm, hbm],
-        out_specs=(vmem, vmem),
+        out_specs=vmem,
         scratch_shapes=[
             pltpu.VMEM((9, 4, V, QW), BF16),
             pltpu.VMEM((8, V, QW), BF16),
@@ -654,10 +669,10 @@
             dma((5,)),
             dma((4, 2)),
             dma((8, 4)),
-            dma((8,)),
+            dma((8, 2)),
             dma((8, 4)),
             dma((9, 4)),
-            dma((8,)),
+            dma((8, 2)),
             dma((3,)),
             dma((3,)),
             dma((2, 2)),
@@ -675,11 +690,14 @@
     )(occ_energy, factors, vir_energy.reshape(1, V), metric)
     gamma, density = pl.pallas_call(
         hand_over,
-        out_shape=outs,
-        in_specs=[vmem, vmem],
+        out_shape=(
+            jax.ShapeDtypeStruct((4 * QW, 128), F32),
+            jax.ShapeDtypeStruct((8, V), F32),
+        ),
+        in_specs=[vmem],
         out_specs=(vmem, vmem),
         compiler_params=pltpu.CompilerParams(vmem_limit_bytes=4 * 1024 * 1024),
-    )(gamma, density)
+    )(both)
     return gamma.reshape(QW, 1, V), density
 
 

time: 116 us -> 116 us (level)
  no operation moved by 1% of the time
where the time goes in v4:
time: 116 us; the launch traced here: 115 us
  Pallas kernels  114 us (98%)
    pallas_call x1, Pallas kernels, per_device(): pl.pallas_call(kernel, out_shape=jax.ShapeDtypeStruct((4 * QW + 32, 128),...  113 us

profile of v4, /device:TPU:1, one launch (start us, length us, event | category | flops | bytes accessed | tf_op | source)
XLA Modules:
  0.0 115.4 jit_solution(1081850156225480168)
XLA Ops:
  0.6 112.8 %shard_map.59.both_ref = f32[1056,128]{1,0:T(8,128)} custom-call(f32[64]{0:T(128)} %occ_ref.1, bf16[1,512,256]{2,1,0:T(8,128)(2,1)} %f_ref.1, f32[1,512]{1,0:T(1,128)} %bitcast.2, f32[1024,1024]{1,0:T(8,128)} %metric_ref.1), custom_call_target="tpu_custom_call" | custom-call | tf_op jit(solution)/shard_map/pallas_call | solution.py:637
  113.5 0.0 copy-start
  113.5 1.0 copy-done
  114.5 0.8 shard_map.60
Async XLA Ops:
  113.5 1.0 copy-start

commit v5 on v4

--- a/solution.py
+++ b/solution.py
@@ -64,6 +64,8 @@
     tail_rsem,
     half_ssem,
     half_rsem,
+    hand_ssem,
+    hand_rsem,
     y_ssem,
     y_rsem,
     z_ssem,
@@ -371,65 +373,117 @@
             for q in range(4):
                 g_acc[q, rows, :] += dot(ub, jb[entry, q], NN)
 
+    def both_ways(d, q, left4):
+        relay(2 * d - 1, q, left4)
+        relay(2 * d, q, left4)
+
+    def far_rows(d, q):
+        for p in (2 * d - 1, 2 * d):
+            to_far_row(slot_of(p), q).start()
+
+    @pl.when(x_hi == 0)
+    def _():
+        for q in (2, 3):
+            arrived(z, q)
+            for way in (1, 0):
+                ring_start(q, way, jb.at[z, q], q).start()
+        for p in (5, 6, 7):
+            relay_r(p)
+            rows_r(p)
+
+    def handed(i):
+        return remote(
+            jb.at[slot_of(i + 1)], jb.at[9 + i], hand_ssem.at[i], hand_rsem.at[i], (b, mate)
+        )
+
     def place(p, carry):
-        slot = slot_of(p)
-
-        @pl.when((p == 0) & (x_hi == 0))
-        def _():
-            for q in (2, 3):
-                arrived(z, q)
-                for way in (1, 0):
-                    ring_start(q, way, jb.at[z, q], q).start()
-            for n in (5, 6):
-                relay_r(n)
-                rows_r(n)
-
-        @pl.when((p == 1) & (x_hi == 0))
-        def _():
-            relay_r(7)
-            rows_r(7)
-
-        @pl.when((p > 0) & (x_hi == 0))
-        def _():
-            relay(p, 2, 1)
-            relay(p, 3, 0)
-
-        @pl.when((p < 5) & (s == 2))
-        def _():
-            relay(p + 3, 2, 0)
-            to_far_row(slot_of(p + 3), 2).start()
-
-        @pl.when((p < 7) & (s == 2))
+        d = (p + 1) // 2
+        n = p - 1
+        slot = slot_of(n)
+
+        @pl.when((p < 7) & (p % 2 == 1) & (x_hi == 0))
+        def _():
+            both_ways(d, 2, 1)
+
+        @pl.when((p < 7) & (p % 2 == 0) & (x_hi == 0))
+        def _():
+            both_ways(d, 3, 0)
+
+        @pl.when((p == 8) & (x_hi == 0))
+        def _():
+            arrived(slot, 2)
+            arrived(slot, 3)
+
+        @pl.when((p < 7) & (p % 2 == 1) & (s == 2))
+        def _():
+            both_ways(d, 0, 1)
+            far_rows(d, 0)
+
+            @pl.when(d < 3)
+            def _():
+                both_ways(d + 1, 2, 0)
+                far_rows(d + 1, 2)
+
+            @pl.when(d == 3)
+            def _():
+                relay(7, 2, 0)
+                to_far_row(slot_of(7), 2).start()
+
+        @pl.when((p < 7) & (p % 2 == 0) & (s == 2))
+        def _():
+            both_ways(d, 1, 1)
+            far_rows(d, 1)
+            both_ways(d, 3, 0)
+
+        @pl.when((p == 7) & (s == 2))
         def _():
             for q in (0, 1):
-                relay(p + 1, q, 1)
-                to_far_row(slot_of(p + 1), q).start()
-
-        @pl.when((p > 0) & (s == 2))
-        def _():
-            relay(p, 3, 0)
-
-        @pl.when(x_hi == 0)
+                relay(7, q, 1)
+                to_far_row(slot_of(7), q).start()
+
+        @pl.when((p == 8) & (s == 2))
+        def _():
+            relay(7, 3, 0)
+
+        @pl.when((p < 9) & (x_hi == 0))
         def _():
             arrived(slot, 0)
             arrived(slot, 1)
 
-        @pl.when((p > 0) & (s == 3))
+        @pl.when((n > 3) & (n < 8) & (s == 3))
         def _():
             for q in (2, 0, 1):
                 arrived(slot, q)
 
+        @pl.when((n > 7) & (s == 2))
+        def _():
+            handed(n - 8).wait_recv()
+
+        block = jnp.where(n > 7, slot_of(n - 7), slot)
         shift = jnp.where(s == 0, -1, jnp.where(s == 1, 1, 0))
-        shift = jnp.where(s == 3, jnp.where(slot > z, -2, 2), shift)
-        other = ((b // 8 + shift + 8) % 8) * 8 + slot
-
-        @pl.when((p > 0) | (s != 3))
-        def _():
-            pair(jnp.where((p == 0) & (s == 2), 8, slot), other)
+        shift = jnp.where((s == 3) | (n > 7), jnp.where(block > z, -2, 2), shift)
+        other = ((b // 8 + shift + 8) % 8) * 8 + block
+        entry = jnp.where((n == 0) & (s == 2), 8, jnp.where(n > 7, n + 1, slot))
+
+        @pl.when(((s != 3) & (n < 8)) | ((s == 3) & (n > 3) & (n < 8)) | ((s == 2) & (n > 7)))
+        def _():
+            pair(entry, other)
 
         return carry
 
-    lax.fori_loop(0, 8, place, 0)
+    @pl.when(s == 3)
+    def _():
+        for i in range(3):
+            for q in (2, 0, 1):
+                arrived(slot_of(i + 1), q)
+            handed(i).start()
+
+    lax.fori_loop(1, 12, place, 0)
+
+    @pl.when(s == 3)
+    def _():
+        for i in range(3):
+            handed(i).wait_send()
 
     sends = []
 
@@ -640,7 +694,7 @@
         in_specs=[hbm, hbm, hbm, hbm],
         out_specs=vmem,
         scratch_shapes=[
-            pltpu.VMEM((9, 4, V, QW), BF16),
+            pltpu.VMEM((12, 4, V, QW), BF16),
             pltpu.VMEM((8, V, QW), BF16),
             pltpu.VMEM((4, V, QW), F32),
             pltpu.VMEM((2, V, QW), F32),
@@ -677,6 +731,8 @@
             dma((3,)),
             dma((2, 2)),
             dma((2, 2)),
+            dma((3,)),
+            dma((3,)),
             dma((4,)),
             dma((4,)),
             dma((8,)),

time: 116 us -> 114 us (0.983)
  Pallas kernels: 114 us -> 112 us
    pallas_call x1, Pallas kernels: 113 us -> 111 us  [per_device(): pl.pallas_call(kernel, out_shape=jax.ShapeDtypeStruct((4 * QW + 32, 128),...]
where the time goes in v5:
time: 114 us
  Pallas kernels  112 us (98%)
    pallas_call x1, Pallas kernels, per_device(): pl.pallas_call(kernel, out_shape=jax.ShapeDtypeStruct((4 * QW + 32, 128),...  111 us

profile of v5, /device:TPU:1, one launch (start us, length us, event | category | flops | bytes accessed | tf_op | source)
XLA Modules:
  0.0 113.9 jit_solution(9049511399818654094)
XLA Ops:
  0.6 111.4 %shard_map.59.both_ref = f32[1056,128]{1,0:T(8,128)} custom-call(f32[64]{0:T(128)} %occ_ref.1, bf16[1,512,256]{2,1,0:T(8,128)(2,1)} %f_ref.1, f32[1,512]{1,0:T(1,128)} %bitcast.2, f32[1024,1024]{1,0:T(8,128)} %metric_ref.1), custom_call_target="tpu_custom_call" | custom-call | tf_op jit(solution)/shard_map/pallas_call | solution.py:691
  112.1 0.0 copy-start
  112.1 1.0 copy-done
  113.1 0.8 shard_map.60
Async XLA Ops:
  112.1 1.0 copy-start
